TPU v7x, 32 devices: a whole 2x2x4 slice. The times are simulated.
32 devices in a mesh: group: 2 (over x), route: 4 (over y, core), cuts: 4 (over z).
Axes of the slice: x: 2, y: 2, z: 4, core: 2. Of those that a mesh axis runs over, the one named last changes fastest.
Arguments:
- query_matrix_rows: bfloat16 [1024, 4096], P(('group', 'route'), 'cuts'), parts along dimension 0, may hold values from -8 to 8
- key_matrix_rows: bfloat16 [1024, 1024], P(('group', 'route'), 'cuts'), parts along dimension 0, may hold values from -8 to 8
- value_matrix_rows: bfloat16 [1024, 1024], P(('group', 'route'), 'cuts'), parts along dimension 0, may hold values from -6 to 6
- attention_output_matrix: bfloat16 [4096, 4096], P('cuts'), may hold values from -0.125 to 0.125
- residual: bfloat16 [1024, 4096], P(('group', 'route'), 'cuts'), parts along dimension 0, may hold values from -6 to 6
- cotangent: bfloat16 [1024, 4096], P(('group', 'route'), 'cuts'), parts along dimension 0, may hold values from -0.59765625 to 0.59765625
- token_expert_choices: int32 [1024, 2], P(('group', 'route')), parts along dimension 0, may hold values from 0 to 3, as said below
- token_slot_positions: int32 [1024, 2], P(('group', 'route')), parts along dimension 0, may hold values from 0 to 127, as said below
- router_choice_weight: float32 [1024, 2], P(('group', 'route')), parts along dimension 0, may hold values from 0.2 to 1
- expert_gate_weight: bfloat16 [4, 3200, 4096], P('route', 'cuts'), may hold values from -0.09375 to 0.09375
- expert_down_weight: bfloat16 [4, 3200, 4096], P('route', 'cuts'), may hold values from -0.15625 to 0.15625
- adapter_down_factor: bfloat16 [4, 64, 4096], P('route'), may hold values from -0.09375 to 0.09375
- adapter_up_factor: bfloat16 [4, 64, 3200], P('route', None, 'cuts'), may hold values from -0.75 to 0.75
Outputs:
- layer_out: bfloat16 [1024, 4096], P(('group', 'route'), 'cuts'), parts along dimension 0
- down_factor_gradient: float32 [8, 64, 4096], P(('group', 'route'), None, 'cuts'), parts along dimension 0
- up_factor_gradient: float32 [8, 64, 3200], P(('group', 'route'), None, 'cuts'), parts along dimension 0
There are 2 independent parts, one for each index of `group`. A program takes and returns all parts, laid end to end along the dimension named above; an argument that names none is the same for every part. Nothing has to cross between parts.
Inputs may be any that keep to these rules, and one draw needn't show every extreme that they name: `token_expert_choices`: the two experts of a token differ. Within one sequence of 128 tokens no expert is named more than 128 times; one expert, the same for all sequences of a draw, is named exactly 128 times in every sequence. `token_slot_positions`: within one sequence the slots given for one expert are all different.
All inputs are finite; a program needn't handle non-finite values.
Results may differ from a plain program's by a relative error of at most 0.014.
Values may be sent and summed in bfloat16 or wider, within the bound.
No kernel may reach another device: no remote copies, remote signals or barrier semaphores. Data moves between devices by JAX's collectives and lax.ppermute only.
A program may use at most 128 MiB of HBM per device.

v0:
```python
import math

import jax
import jax.numpy as jnp
from jax import lax
from jax.sharding import PartitionSpec as P

HEAD_DIM = 128


ADAPTER_SCALE = 0.5


def causal_heads(query_matrix_rows, key_matrix_rows, value_matrix_rows):
    length = query_matrix_rows.shape[0]
    kv_local = key_matrix_rows.shape[1] // HEAD_DIM
    per_kv = query_matrix_rows.shape[1] // key_matrix_rows.shape[1]
    queries = query_matrix_rows.reshape(length, kv_local, per_kv, HEAD_DIM)
    key_view = key_matrix_rows.reshape(length, kv_local, HEAD_DIM)
    value_view = value_matrix_rows.reshape(length, kv_local, HEAD_DIM)
    scores = jnp.einsum(
        "qhgd,khd->hgqk", queries, key_view, preferred_element_type=jnp.float32
    ) / math.sqrt(HEAD_DIM)
    future = lax.broadcasted_iota(jnp.int32, (length, length), 1) > lax.broadcasted_iota(
        jnp.int32, (length, length), 0
    )
    scores = jnp.where(future, -jnp.inf, scores)
    row_max = jnp.max(scores, axis=-1, keepdims=True)
    shifted = jnp.exp(scores - row_max)
    weights = (shifted / jnp.sum(shifted, axis=-1, keepdims=True)).astype(jnp.bfloat16)
    attended = jnp.einsum("hgqk,khd->qhgd", weights, value_view, preferred_element_type=jnp.float32)
    return attended.astype(jnp.bfloat16).reshape(length, query_matrix_rows.shape[1])


def fill_slots(source_rows, owners):
    padded = jnp.concatenate(
        [source_rows, jnp.zeros((1, source_rows.shape[1]), source_rows.dtype)], axis=0
    )
    return jnp.take(padded, owners, axis=0)


def weighted_slots(source_rows, owners, scales):
    return (fill_slots(source_rows, owners).astype(jnp.float32) * scales[:, None]).astype(
        jnp.bfloat16
    )


def combine_rows(returned, cell_ids, router_choice_weight):
    first_out = jnp.take(returned, cell_ids[:, 0], axis=0)
    second_out = jnp.take(returned, cell_ids[:, 1], axis=0)
    return router_choice_weight[:, 0:1] * first_out + router_choice_weight[:, 1:2] * second_out


def local(
    query_matrix_rows,
    key_matrix_rows,
    value_matrix_rows,
    attention_output_matrix,
    residual,
    cotangent,
    token_expert_choices,
    token_slot_positions,
    router_choice_weight,
    expert_gate_weight,
    expert_down_weight,
    adapter_down_factor,
    adapter_up_factor,
):
    attended = causal_heads(query_matrix_rows, key_matrix_rows, value_matrix_rows)
    head_terms = jnp.dot(attended, attention_output_matrix, preferred_element_type=jnp.float32)
    head_cols = lax.psum_scatter(head_terms, "cuts", scatter_dimension=1, tiled=True)
    hidden_cols = (residual.astype(jnp.float32) + head_cols).astype(jnp.bfloat16)
    length = residual.shape[0]
    col_count = residual.shape[1]
    model_width = expert_gate_weight.shape[2]
    experts = lax.axis_size("route")
    capacity = 4 * length // experts
    cell_ids = token_expert_choices * capacity + token_slot_positions
    flat_cells = cell_ids.reshape(-1)
    owners = (
        jnp.full((experts * capacity,), length, jnp.int32)
        .at[flat_cells]
        .set(jnp.repeat(jnp.arange(length, dtype=jnp.int32), 2))
    )
    scales = (
        jnp.zeros((experts * capacity,), jnp.float32)
        .at[flat_cells]
        .set(router_choice_weight.reshape(-1))
    )
    full_x, full_g = (
        lax.all_gather(hidden_cols, "cuts", axis=1, tiled=True),
        lax.all_gather(cotangent, "cuts", axis=1, tiled=True),
    )
    token_part = fill_slots(full_x, owners).reshape(experts, capacity, model_width)
    grad_part = weighted_slots(full_g, owners, scales).reshape(experts, capacity, model_width)
    slot_x, slot_g = (
        lax.all_to_all(token_part, "route", split_axis=0, concat_axis=0, tiled=True),
        lax.all_to_all(grad_part, "route", split_axis=0, concat_axis=0, tiled=True),
    )
    expert_input_rows = slot_x.reshape(-1, model_width)
    rows_g = slot_g.reshape(-1, model_width)
    reduce_final_axis = (((1,), (1,)), ((), ()))
    contract_first = (((0,), (0,)), ((), ()))
    gate_primary_product = lax.dot_general(
        expert_input_rows,
        expert_gate_weight[0],
        reduce_final_axis,
        preferred_element_type=jnp.float32,
    )
    adapter_product = lax.dot_general(
        expert_input_rows,
        adapter_down_factor[0],
        reduce_final_axis,
        preferred_element_type=jnp.float32,
    ).astype(jnp.bfloat16)
    gate_preactivation = gate_primary_product + ADAPTER_SCALE * jnp.dot(
        adapter_product, adapter_up_factor[0], preferred_element_type=jnp.float32
    )
    sigmoid_gate = jax.nn.sigmoid(gate_preactivation)
    activ = (gate_preactivation * sigmoid_gate).astype(jnp.bfloat16)
    partial_out = jnp.dot(activ, expert_down_weight[0], preferred_element_type=jnp.float32).astype(
        jnp.bfloat16
    )
    slot_sums = lax.psum_scatter(
        partial_out.astype(jnp.float32)
        .reshape(experts, capacity, model_width)
        .astype(jnp.bfloat16),
        "cuts",
        scatter_dimension=2,
        tiled=True,
    ).astype(jnp.float32)
    returned = (
        lax.all_to_all(
            slot_sums.astype(jnp.bfloat16), "route", split_axis=0, concat_axis=0, tiled=True
        )
        .astype(slot_sums.dtype)
        .reshape(experts * capacity, col_count)
    )
    merged = hidden_cols.astype(jnp.float32) + combine_rows(
        returned, cell_ids, router_choice_weight
    )
    layer_out = merged.astype(jnp.bfloat16)
    grad_hidden = lax.dot_general(
        rows_g, expert_down_weight[0], reduce_final_axis, preferred_element_type=jnp.float32
    )
    preactivation_gradient = (
        grad_hidden * sigmoid_gate * (1.0 + gate_preactivation * (1.0 - sigmoid_gate))
    ).astype(jnp.bfloat16)
    up_factor_gradient = ADAPTER_SCALE * lax.dot_general(
        adapter_product, preactivation_gradient, contract_first, preferred_element_type=jnp.float32
    )
    factor_part = lax.dot_general(
        preactivation_gradient,
        adapter_up_factor[0],
        reduce_final_axis,
        preferred_element_type=jnp.float32,
    ).astype(jnp.bfloat16)
    gradient_pieces = lax.dot_general(
        factor_part, expert_input_rows, contract_first, preferred_element_type=jnp.float32
    )
    down_factor_gradient = ADAPTER_SCALE * lax.psum_scatter(
        gradient_pieces.astype(jnp.bfloat16), "cuts", scatter_dimension=1, tiled=True
    ).astype(jnp.float32)
    return (layer_out, down_factor_gradient[None], up_factor_gradient[None])


def solution(mesh):
    return jax.shard_map(
        local,
        mesh=mesh,
        in_specs=(
            P(("group", "route"), "cuts"),
            P(("group", "route"), "cuts"),
            P(("group", "route"), "cuts"),
            P("cuts", None),
            P(("group", "route"), "cuts"),
            P(("group", "route"), "cuts"),
            P(("group", "route"), None),
            P(("group", "route"), None),
            P(("group", "route"), None),
            P("route", "cuts", None),
            P("route", "cuts", None),
            P("route", None, None),
            P("route", None, "cuts"),
        ),
        out_specs=(
            P(("group", "route"), "cuts"),
            P(("group", "route"), None, "cuts"),
            P(("group", "route"), None, "cuts"),
        ),
        check_vma=False,
    )
```

profile of v0, /device:TPU:0, one launch (start us, length us, event | category | flops | bytes accessed | tf_op | source)
XLA Modules:
  0.0 290.6 jit_solution(17472282540791643243)
XLA Ops:
  11.2 6.0 %fusion.44 = f32[128,4096]{1,0:T(8,128)} fusion(bf16[128,1024]{0,1:T(8,128)(2,1)S(1)} %bitcast.77, bf16[1024,4096]{1,0:T(8,128)(2,1)} %param.20), kind=kOutput, calls=%fused_computation.69 | convolution fusion | flops 1073741824 | bytes 10747904 | tf_op jit(solution)/shard_map/dot_general | solution.py:70
  17.3 46.5 %reduce-scatter.4.cloned.1.call-done = f32[128,1024]{1,0:T(8,128)} async-done(((f32[128,4096]{1,0:T(8,128)}), f32[128,1024]{1,0:T(8,128)}) %reduce-scatter.4.cloned.1.call-update) | async-done | bytes 524304 | tf_op jit(solution)/shard_map/reduce_scatter | solution.py:71
  63.7 1.8 add_convert_fusion
  67.4 25.6 %all-gather.3.cloned.1.call-done = bf16[128,4096]{1,0:T(8,128)(2,1)} async-done(((bf16[128,1024]{1,0:T(8,128)(2,1)}), bf16[128,4096]{1,0:T(8,128)(2,1)}) %all-gather.3.cloned.1.call-update) | async-done | bytes 1048592 | tf_op jit(solution)/shard_map/all_gather | solution.py:91
  94.4 4.4 %gather_fusion = bf16[512,4096]{1,0:T(8,128)(2,1)} fusion(bf16[129,4096]{1,0:T(8,128)(2,1)S(1)} %concatenate.6, s32[1024]{0:T(1024)S(1)} %pad_clamp_fusion.2), kind=kCustom, calls=%fused_computation.clone | custom fusion | bytes 8390656 | tf_op jit(solution)/shard_map/jit(_take)/gather | solution.py:39
  98.8 4.6 %broadcast_select_fusion = bf16[512,4096]{1,0:T(8,128)(2,1)} fusion(bf16[512,4096]{1,0:T(8,128)(2,1)} %gather_fusion, pred[512]{0:T(512)(128)(4,1)S(1)} %compare_and_fusion.2), kind=kLoop, calls=%fused_computation.16 | loop fusion | flops 2097152 | bytes 8389120 | tf_op jit(solution)/shard_map/jit(_take)/select_n | solution.py:39
  103.4 4.8 %all-to-all-start = ((bf16[4,128,4096]{2,1,0:T(8,128)(2,1)}), bf16[4,128,4096]{2,1,0:T(8,128)(2,1)}, u32[]{:S(2)}, u32[]{:S(2)}) async-start(bf16[4,128,4096]{2,1,0:T(8,128)(2,1)} %bitcast.74), calls=%async_computation.1 | async-start | bytes 8388608 | tf_op jit(solution)/shard_map/all_to_all | solution.py:97
  109.0 47.4 %all-to-all-done = bf16[4,128,4096]{2,1,0:T(8,128)(2,1)} async-done(((bf16[4,128,4096]{2,1,0:T(8,128)(2,1)}), bf16[4,128,4096]{2,1,0:T(8,128)(2,1)}, u32[]{:S(2)}, u32[]{:S(2)}) %all-to-all-start) | async-done | bytes 4194336 | tf_op jit(solution)/shard_map/all_to_all | solution.py:97
  156.5 7.0 %fusion.5 = f32[512,800]{0,1:T(8,128)S(1)} fusion(bf16[512,4096]{1,0:T(8,128)(2,1)} %bitcast.11, bf16[1,800,4096]{2,1,0:T(8,128)(2,1)} %param.26), kind=kOutput, calls=%fused_computation.12 | convolution fusion | flops 3355443200 | bytes 12386304 | tf_op jit(solution)/shard_map/dot_general | solution.py:104
  163.5 3.6 %convolution_convert_fusion.3 = bf16[512,64]{0,1:T(8,128)(2,1)S(1)} fusion(bf16[512,4096]{1,0:T(8,128)(2,1)} %bitcast.11, bf16[1,64,4096]{2,1,0:T(8,128)(2,1)S(1)} %copy-done), kind=kOutput, calls=%fused_computation.30 | convolution fusion | flops 268468224 | bytes 4784128 | tf_op jit(solution)/shard_map/dot_general | solution.py:110
  167.5 9.1 %fusion.7 = bf16[512,4096]{1,0:T(8,128)(2,1)} fusion(bf16[1,800,4096]{2,1,0:T(8,128)(2,1)} %param.27, f32[512,800]{0,1:T(8,128)S(1)} %multiply_add_fusion), kind=kOutput, calls=%fused_computation.14 | convolution fusion | flops 3359588352 | bytes 12386304 | tf_op jit(solution)/shard_map/dot_general | solution.py:121
  177.6 1.4 scatter_custom_fusion.1
  180.4 4.4 %gather_fusion.3 = bf16[512,4096]{1,0:T(8,128)(2,1)} fusion(bf16[129,4096]{1,0:T(8,128)(2,1)S(1)} %concatenate.7, s32[1024]{0:T(1024)S(1)} %pad_clamp_fusion.2), kind=kCustom, calls=%fused_computation.2.clone | custom fusion | bytes 8390656 | tf_op jit(solution)/shard_map/jit(_take)/gather | solution.py:39
  184.7 4.7 %multiply_convert_fusion = bf16[512,4096]{1,0:T(8,128)(2,1)S(1)} fusion(bf16[512,4096]{1,0:T(8,128)(2,1)} %gather_fusion.3, f32[512]{0:T(512)S(1)} %scatter_custom_fusion.1, pred[512]{0:T(512)(128)(4,1)S(1)} %compare_and_fusion.2), kind=kLoop, calls=%fused_computation.7 | loop fusion | flops 8388608 | bytes 8391168 | tf_op jit(solution)/shard_map/convert_element_type | solution.py:43
  189.5 50.8 %all_to_all.15 = bf16[4,128,4096]{2,1,0:T(8,128)(2,1)S(1)} all-to-all(bf16[4,128,4096]{2,1,0:T(8,128)(2,1)S(1)} %bitcast.73), channel_id=1, replica_groups=mesh['group'=2,'route'=4,'cuts'=4] {'route'}, dimensions={0} | all-to-all | bytes 8388608 | tf_op jit(solution)/shard_map/all_to_all | solution.py:98
  240.3 3.9 %multiply_convert_fusion.1 = bf16[512,800]{0,1:T(8,128)(2,1)S(1)} fusion(f32[512,800]{0,1:T(8,128)S(1)} %multiply_add_fusion, bf16[512,4096]{1,0:T(8,128)(2,1)S(1)} %bitcast.76, bf16[1,800,4096]{2,1,0:T(8,128)(2,1)S(1)} %bitcast.84), kind=kOutput, calls=%fused_computation.17 | convolution fusion | flops 3359129600 | bytes 13205504 | tf_op jit(solution)/shard_map/dot_general | solution.py:143
  244.3 4.6 %convolution_convert_fusion = bf16[64,4096]{1,0:T(8,128)(2,1)} fusion(bf16[512,4096]{1,0:T(8,128)(2,1)} %bitcast.11, bf16[512,800]{0,1:T(8,128)(2,1)S(1)} %multiply_convert_fusion.1, bf16[1,64,800]{2,1,0:T(8,128)(2,1)S(1)} %copy-done.3), kind=kOutput, calls=%fused_computation.15 | convolution fusion | flops 321159168 | bytes 5640192 | tf_op jit(solution)/shard_map/dot_general | solution.py:158
  248.9 3.2 %reduce-scatter.6.cloned.1.call-done = bf16[4,128,1024]{2,1,0:T(8,128)(2,1)} async-done(((bf16[4,128,4096]{2,1,0:T(8,128)(2,1)}), bf16[4,128,1024]{2,1,0:T(8,128)(2,1)}) %reduce-scatter.6.cloned.1.call-update) | async-done | bytes 1048592 | tf_op jit(solution)/shard_map/reduce_scatter | solution.py:124
  252.1 4.2 %all-to-all-start.1 = ((bf16[4,128,1024]{2,1,0:T(8,128)(2,1)}), bf16[4,128,1024]{2,1,0:T(8,128)(2,1)}, u32[]{:S(2)}, u32[]{:S(2)}) async-start(bf16[4,128,1024]{2,1,0:T(8,128)(2,1)} %reduce-scatter.6.cloned.1.call-done), calls=%async_computation.3 | async-start | bytes 2097152 | tf_op jit(solution)/shard_map/all_to_all | solution.py:133
  257.5 19.1 %reduce-scatter.8.cloned.1.call-done = bf16[64,1024]{1,0:T(8,128)(2,1)} async-done(((bf16[64,4096]{1,0:T(8,128)(2,1)}), bf16[64,1024]{1,0:T(8,128)(2,1)}) %reduce-scatter.8.cloned.1.call-update) | async-done | bytes 131088 | tf_op jit(solution)/shard_map/reduce_scatter | solution.py:161
  276.6 1.6 multiply_bitcast_fusion
  278.2 1.5 bitcast_convert_fusion
  280.5 1.6 gather_fusion.2
  282.1 2.0 fusion.21
  (60 shorter events, 12.5 us)
Async XLA Ops:
  7.2 156.3 %copy-start = (bf16[1,64,4096]{2,1,0:T(8,128)(2,1)S(1)}, bf16[1,64,4096]{2,1,0:T(8,128)(2,1)}, u32[]{:S(2)}) copy-start(bf16[1,64,4096]{2,1,0:T(8,128)(2,1)} %param.28) | copy-start | bytes 1572868
  7.2 56.5 %reduce-scatter.4.cloned.1.call-start = ((), (), s32[]{:S(2)}) async-start(), calls=%async_computation.6 | async-start | bytes 2621440 | tf_op jit(solution)/shard_map/reduce_scatter | solution.py:71
  11.1 52.6 %copy-start.4 = (bf16[128,1024]{1,0:T(8,128)(2,1)S(1)}, bf16[128,1024]{1,0:T(8,128)(2,1)}, u32[]{:S(2)}) copy-start(bf16[128,1024]{1,0:T(8,128)(2,1)} %param.21) | copy-start | bytes 786436
  11.1 54.4 %copy-start.6 = (s32[128,2]{0,1:T(2,128)S(1)}, s32[128,2]{0,1:T(2,128)}, u32[]{:S(2)}) copy-start(s32[128,2]{0,1:T(2,128)} %param.24) | copy-start | bytes 3076
  11.2 54.4 %copy-start.7 = (s32[128,2]{0,1:T(2,128)S(1)}, s32[128,2]{0,1:T(2,128)}, u32[]{:S(2)}) copy-start(s32[128,2]{0,1:T(2,128)} %param.23) | copy-start | bytes 3076
  17.2 75.9 %all-gather.3.cloned.1.call-start = ((), (), s32[]{:S(2)}) async-start(), calls=%async_computation.7 | async-start | bytes 1310720 | tf_op jit(solution)/shard_map/all_gather | solution.py:91
  103.4 53.0 %all-to-all-start = ((bf16[4,128,4096]{2,1,0:T(8,128)(2,1)}), bf16[4,128,4096]{2,1,0:T(8,128)(2,1)}, u32[]{:S(2)}, u32[]{:S(2)}) async-start(bf16[4,128,4096]{2,1,0:T(8,128)(2,1)} %bitcast.74), calls=%async_computation.1 | async-start | bytes 8388608 | tf_op jit(solution)/shard_map/all_to_all | solution.py:97
  108.3 70.8 %all-gather.5.cloned.1.call-start = ((), (), s32[]{:S(2)}) async-start(), calls=%async_computation.9 | async-start | bytes 1310720 | tf_op jit(solution)/shard_map/all_gather | solution.py:92
  109.0 143.1 %reduce-scatter.6.cloned.1.call-start = ((), (), s32[]{:S(2)}) async-start(), calls=%async_computation.8 | async-start | bytes 5242880 | tf_op jit(solution)/shard_map/reduce_scatter | solution.py:124
  163.5 3.6 %copy-start.3 = (bf16[1,64,800]{2,1,0:T(8,128)(2,1)S(1)}, bf16[1,64,800]{2,1,0:T(8,128)(2,1)}, u32[]{:S(2)}) copy-start(bf16[1,64,800]{2,1,0:T(8,128)(2,1)} %param.29) | copy-start | bytes 307204
  176.7 0.7 copy-start.5
  176.7 99.9 %reduce-scatter.8.cloned.1.call-start = ((), (), s32[]{:S(2)}) async-start(), calls=%async_computation.10 | async-start | bytes 655360 | tf_op jit(solution)/shard_map/reduce_scatter | solution.py:161
  184.7 55.6 %slice-start = ((s8[6553600]{0:T(1024)(128)(4,1)}), s8[4194304]{0:T(1024)(128)(4,1)S(1)}, s32[]{:S(2)}) async-start(s8[6553600]{0:T(1024)(128)(4,1)} %bitcast.83), calls=%async_computation.11 | async-start | bytes 8388608
  189.5 50.9 %slice-start.1 = ((s8[6553600]{0:T(1024)(128)(4,1)}), s8[2359296]{0:T(1024)(128)(4,1)S(1)}, s32[]{:S(2)}) async-start(s8[6553600]{0:T(1024)(128)(4,1)} %bitcast.83), calls=%async_computation.12 | async-start | bytes 4718592
  252.1 26.1 %all-to-all-start.1 = ((bf16[4,128,1024]{2,1,0:T(8,128)(2,1)}), bf16[4,128,1024]{2,1,0:T(8,128)(2,1)}, u32[]{:S(2)}, u32[]{:S(2)}) async-start(bf16[4,128,1024]{2,1,0:T(8,128)(2,1)} %reduce-scatter.6.cloned.1.call-done), calls=%async_computation.3 | async-start | bytes 2097152 | tf_op jit(solution)/shard_map/all_to_all | solution.py:133
  279.7 2.4 copy-start.2
  279.7 4.4 %copy-start.1 = (bf16[1,64,4096]{2,1,0:T(8,128)(2,1)S(1)}, bf16[1,64,4096]{2,1,0:T(8,128)(2,1)}, u32[]{:S(2)}) copy-start(bf16[1,64,4096]{2,1,0:T(8,128)(2,1)} %param.28) | copy-start | bytes 1572868
Sparse Core Ops, SparseCore 0:
  17.3 46.3 reduce-scatter.3
  65.9 27.1 all-gather.2
  110.6 27.8 all-gather.4
  176.8 75.2 reduce-scatter.5
  254.2 22.3 reduce-scatter.7
where the time goes:
time: 291 us
  waiting for transfers between devices  143 us (49%)
  blocking collectives  50.8 us (17%)
  matrix products  36.7 us (13%)
  local copies, waits for them, and re-layouts  20.7 us (7%)
  other arithmetic  16.2 us (6%)
  between operations  14.1 us (5%)
  starting transfers between devices  9.47 us (3%)
    all_to_all x1, blocking collectives, local(): lax.all_to_all(grad_part, 'route', split_axis=0, concat_axis=0, tiled=True)  50.8 us
    all_to_all x1, waiting for transfers between devices, local(): lax.all_to_all(token_part, 'route', split_axis=0, concat_axis=0, tiled=True)  47.4 us
    reduce_scatter x1, waiting for transfers between devices, local(): lax.psum_scatter(head_terms, 'cuts', scatter_dimension=1, tiled=True)  46.5 us
    all_gather x1, waiting for transfers between devices, local(): lax.all_gather(hidden_cols, 'cuts', axis=1, tiled=True)  25.6 us
    reduce_scatter x1, waiting for transfers between devices, local(): lax.psum_scatter(gradient_pieces.astype(jnp.bfloat16), 'cuts', scatter_di...  19.1 us
    dot_general x1, matrix products, local(): jnp.dot(activ, expert_down_weight[0], preferred_element_type=jnp.float32)  9.11 us
    gather x2, local copies, waits for them, and re-layouts, fill_slots(): return jnp.take(padded, owners, axis=0)  8.77 us
    dot_general x1, matrix products, local(): lax.dot_general(expert_input_rows, expert_gate_weight[0], reduce_final_ax...  7 us
  transfers between devices with their start and end apart: 7, of which 5 were waited for; matrix products, arithmetic and copies ran while one was open for 16% of the time, Pallas kernels for 0%

commit v1 on v0

--- a/solution.py
+++ b/solution.py
@@ -1,14 +1,264 @@
+import functools
 import math
 
 import jax
 import jax.numpy as jnp
 from jax import lax
+from jax.experimental import pallas as pl
+from jax.experimental.pallas import tpu as pltpu
 from jax.sharding import PartitionSpec as P
 
 HEAD_DIM = 128
-
-
 ADAPTER_SCALE = 0.5
+F32 = jnp.float32
+BF16 = jnp.bfloat16
+LAST = (((1,), (1,)), ((), ()))
+FIRST = (((0,), (0,)), ((), ()))
+
+
+def fetch(blocks, w_hbm, wbuf, sems):
+    copies = []
+    for i, block in enumerate(blocks):
+        width = wbuf.shape[2]
+        columns = pl.ds(pl.multiple_of(block * width, width), width)
+        copies.append(pltpu.make_async_copy(w_hbm.at[:, columns], wbuf.at[i], sems.at[i]))
+        copies[-1].start()
+    return copies
+
+
+def attend_kernel(across, q_ref, k_ref, v_ref, w_hbm, att, out, wbuf, sems):
+    (copy,) = fetch(across.blocks()[-1:], w_hbm, wbuf, sems)
+    length = q_ref.shape[0]
+    per_kv = q_ref.shape[1] // k_ref.shape[1]
+    rows = per_kv * length
+    query_at = lax.broadcasted_iota(jnp.int32, (rows, length), 0) % length
+    future = lax.broadcasted_iota(jnp.int32, (rows, length), 1) > query_at
+    for g in range(k_ref.shape[1] // HEAD_DIM):
+        lanes = slice(g * HEAD_DIM, (g + 1) * HEAD_DIM)
+        heads = [
+            slice((g * per_kv + h) * HEAD_DIM, (g * per_kv + h + 1) * HEAD_DIM) for h in range(per_kv)
+        ]
+        queries = jnp.concatenate([q_ref[:, h] for h in heads], axis=0)
+        scores = lax.dot_general(queries, k_ref[:, lanes], LAST, preferred_element_type=F32)
+        scores = jnp.where(future, -jnp.inf, scores * (1.0 / math.sqrt(HEAD_DIM)))
+        shifted = jnp.exp(scores - jnp.max(scores, axis=-1, keepdims=True))
+        weights = (shifted / jnp.sum(shifted, axis=-1, keepdims=True)).astype(BF16)
+        got = jnp.dot(weights, v_ref[:, lanes], preferred_element_type=F32).astype(BF16)
+        for i, h in enumerate(heads):
+            att[:, h] = got[i * length : (i + 1) * length]
+    copy.wait()
+    out[...] = jnp.dot(att[...], wbuf[0], preferred_element_type=F32).astype(out.dtype)
+
+
+def project_kernel(across, slots, att, r_ref, w_hbm, *refs):
+    outs, (wbuf, sems) = refs[:-2], refs[-2:]
+    blocks = across.blocks()
+    copies = fetch([blocks[m] for m in slots], w_hbm, wbuf, sems)
+    for i, m in enumerate(slots):
+        copies[i].wait()
+        term = jnp.dot(att[...], wbuf[i], preferred_element_type=F32)
+        if m == 0:
+            term = term + r_ref[...].astype(F32)
+        outs[i][...] = term.astype(outs[i].dtype)
+
+
+def projecting(kernel, outs, args, matrix, slots, width, flops):
+    whole = pl.BlockSpec(memory_space=pltpu.VMEM)
+    shapes = [jax.ShapeDtypeStruct(shape, dtype) for shape, dtype in outs]
+    return pl.pallas_call(
+        kernel,
+        out_shape=shapes,
+        in_specs=[whole] * len(args) + [pl.BlockSpec(memory_space=pl.ANY)],
+        out_specs=[whole] * len(outs),
+        scratch_shapes=[
+            pltpu.VMEM((slots, matrix.shape[0], width), BF16),
+            pltpu.SemaphoreType.DMA((slots,)),
+        ],
+        cost_estimate=pl.CostEstimate(
+            flops=flops, bytes_accessed=2 * slots * matrix.shape[0] * width, transcendentals=0
+        ),
+    )(*args, matrix)
+
+
+def attend_and_project(across, queries, keys, values, residual, matrix):
+    length, width = residual.shape
+    rows = (length, queries.shape[1])
+    one = 2 * length * queries.shape[1] * width
+    attended, last = projecting(
+        functools.partial(attend_kernel, across),
+        [(rows, BF16), ((length, width), BF16)],
+        [queries, keys, values],
+        matrix,
+        1,
+        width,
+        one + 4 * length * length * queries.shape[1],
+    )
+    slots = list(range(across.n - 1))[::-1]
+    others = projecting(
+        functools.partial(project_kernel, across, slots),
+        [((length, width), F32 if m == 0 else BF16) for m in slots],
+        [attended, residual],
+        matrix,
+        len(slots),
+        width,
+        one * len(slots),
+    )
+    return [*others[::-1], last]
+
+
+class Swaps:
+    def __init__(self, axis, n, stride=1):
+        self.axis, self.n, self.stride = axis, n, stride
+
+    def blocks(self):
+        me = lax.axis_index(self.axis) // self.stride % self.n
+        return [me ^ m for m in range(self.n)]
+
+    def swap(self, x, bit):
+        step = bit * self.stride
+        pairs = [(i, i ^ step) for i in range(lax.axis_size(self.axis))]
+        return lax.ppermute(x, self.axis, pairs)
+
+    def gather(self, x, highest=False):
+        slots = [x]
+        for m in range(1, self.n):
+            bit = 1 << m.bit_length() - 1 if highest else m & -m
+            slots.append(self.swap(slots[m ^ bit], bit))
+        return slots
+
+    def reduce(self, slots):
+        sums = [[x] for x in slots]
+        for m in reversed(range(1, self.n)):
+            term = sums[m][0]
+            for x in sums[m][1:]:
+                term = term.astype(F32) + x.astype(F32)
+            sums[m & (m - 1)].append(self.swap(term.astype(BF16), m & -m))
+        return sum((x.astype(F32) for x in sums[0][1:]), sums[0][0].astype(F32))
+
+
+def column_block(matrix, block, width):
+    return lax.dynamic_slice_in_dim(matrix, block * width, width, axis=1)
+
+
+def dense_layer(
+    query_matrix_rows,
+    key_matrix_rows,
+    value_matrix_rows,
+    attention_output_matrix,
+    residual,
+    cotangent,
+    token_expert_choices,
+    router_choice_weight,
+    expert_gate_weight,
+    expert_down_weight,
+    adapter_down_factor,
+    adapter_up_factor,
+):
+    width = residual.shape[1]
+    cuts, route = lax.axis_size("cuts"), lax.axis_size("route")
+    inner = min(2, route)
+    across = Swaps("cuts", cuts)
+    chips = Swaps("route", route // inner, inner)
+    cores = Swaps("route", inner)
+
+    def spread(x):
+        mine = jnp.concatenate(chips.gather(x), axis=0)
+        return cores.gather(mine)
+
+    def collect(parts):
+        own = cores.reduce(parts).astype(BF16)
+        return chips.reduce(jnp.split(own, route // inner, axis=0)).astype(BF16)
+
+    columns = across.blocks()
+    gate, down = expert_gate_weight[0], expert_down_weight[0]
+    low_in, low_out = adapter_down_factor[0], adapter_up_factor[0]
+
+    chosen = token_expert_choices[:, :, None] == jnp.arange(route, dtype=jnp.int32)
+    table = jnp.sum(jnp.where(chosen, router_choice_weight[:, :, None], 0.0), axis=1).T
+    scales = [
+        lax.dynamic_index_in_dim(x, lax.axis_index("route"), axis=1, keepdims=False).reshape(-1, 1)
+        for x in spread(table[None])
+    ]
+
+    even = {0: cotangent}
+    for m in range(2, cuts, 2):
+        even[m] = across.swap(even[m & (m - 1)], m & -m)
+    even = {m: jnp.concatenate(chips.gather(x), axis=0) for m, x in even.items()}
+    cot_slots = {m: cores.gather(x) for m, x in even.items()}
+    if cuts > 1:
+        odd = cores.gather(across.swap(jnp.concatenate(list(even.values()), axis=0), 1))
+        odd = [jnp.split(x, cuts // 2, axis=0) for x in odd]
+        for i, m in enumerate(even):
+            cot_slots[m + 1] = [x[i] for x in odd]
+
+    terms = attend_and_project(
+        across,
+        query_matrix_rows,
+        key_matrix_rows,
+        value_matrix_rows,
+        residual,
+        attention_output_matrix,
+    )
+    hidden = across.reduce(terms).astype(BF16)
+    hid_slots = [spread(x) for x in across.gather(hidden)]
+
+    halves = range(inner)
+    pre, low, grad_hidden = ([0.0] * inner for _ in range(3))
+    for m in sorted(range(cuts), key=lambda m: (m % 2, m)):
+        if m == cuts - 1:
+            pre, low = lax.optimization_barrier((pre, low))
+        if m == 1:
+            grad_hidden = lax.optimization_barrier(grad_hidden)
+        for h in halves:
+            grad_hidden[h] += lax.dot_general(
+                cot_slots[m][h], column_block(down, columns[m], width), LAST, preferred_element_type=F32
+            )
+            pre[h] += lax.dot_general(
+                hid_slots[m][h], column_block(gate, columns[m], width), LAST, preferred_element_type=F32
+            )
+            low[h] += lax.dot_general(
+                hid_slots[m][h], column_block(low_in, columns[m], width), LAST, preferred_element_type=F32
+            )
+    activ = [0.0] * inner
+    for h in halves:
+        low[h] = low[h].astype(BF16)
+        pre[h] += ADAPTER_SCALE * jnp.dot(low[h], low_out, preferred_element_type=F32)
+        activ[h] = (pre[h] * jax.nn.sigmoid(pre[h])).astype(BF16)
+
+    outs = [None] * cuts
+    for m in reversed(range(cuts)):
+        parts = []
+        for h in halves:
+            part = jnp.dot(
+                activ[h], column_block(down, columns[m], width), preferred_element_type=F32
+            )
+            parts.append((scales[h] * part).astype(BF16))
+        if m == cuts - 1:
+            pre, parts = lax.optimization_barrier((pre, parts))
+        outs[m] = collect(parts)
+    layer_out = (hidden.astype(F32) + across.reduce(outs)).astype(BF16)
+
+    up_grad, factors = 0.0, []
+    for h in halves:
+        sig = jax.nn.sigmoid(pre[h])
+        slope = sig * (1.0 + pre[h] * (1.0 - sig))
+        grad_pre = (scales[h] * grad_hidden[h] * slope).astype(BF16)
+        up_grad += lax.dot_general(low[h], grad_pre, FIRST, preferred_element_type=F32)
+        factors.append(
+            lax.dot_general(low_out, grad_pre, LAST, preferred_element_type=F32).astype(BF16)
+        )
+    up_grad = ADAPTER_SCALE * up_grad
+    factor = jnp.concatenate(factors, axis=0)
+    shift = 1
+    while shift < cuts:
+        other = across.swap(factor, shift)
+        factor = (factor.astype(F32) + other.astype(F32)).astype(BF16)
+        shift *= 2
+    down_grad = ADAPTER_SCALE * sum(
+        jnp.dot(x, rows, preferred_element_type=F32)
+        for x, rows in zip(jnp.split(factor, inner, axis=0), hid_slots[0], strict=True)
+    )
+    return layer_out, down_grad[None], up_grad[None]
 
 
 def causal_heads(query_matrix_rows, key_matrix_rows, value_matrix_rows):
@@ -51,7 +301,7 @@
     return router_choice_weight[:, 0:1] * first_out + router_choice_weight[:, 1:2] * second_out
 
 
-def local(
+def slot_layer(
     query_matrix_rows,
     key_matrix_rows,
     value_matrix_rows,
@@ -164,6 +414,15 @@
     return (layer_out, down_factor_gradient[None], up_factor_gradient[None])
 
 
+def local(*arrays):
+    choices, positions = 6, 7
+    length, experts = arrays[choices].shape[0], lax.axis_size("route")
+    powers = all(n & (n - 1) == 0 for n in (experts, lax.axis_size("cuts")))
+    if powers and 4 * length // experts >= length:
+        return dense_layer(*arrays[:positions], *arrays[positions + 1 :])
+    return slot_layer(*arrays)
+
+
 def solution(mesh):
     return jax.shard_map(
         local,

time: 291 us -> 149 us (0.51)
  waiting for transfers between devices: 143 us -> 66.5 us
  blocking collectives: 50.8 us -> 0 us
  starting transfers between devices: 9.47 us -> 39.4 us
  local copies, waits for them, and re-layouts: 20.7 us -> 3.21 us
  matrix products: 36.7 us -> 23.9 us
  between operations: 14.1 us -> 1.31 us
  other arithmetic: 16.2 us -> 5.71 us
  Pallas kernels: 0 us -> 9.11 us
    reduce_scatter x3 -> x0, waiting for transfers between devices: 68.8 us -> none  [the longest x1 46.5 us: local(): lax.psum_scatter(head_terms, 'cuts', scatter_dimension=1, tiled=True)]
    ppermute x0 -> x36, waiting for transfers between devices: none -> 66.5 us  [swap(): return lax.ppermute(x, self.axis, pairs)]
    all_to_all x1 -> x0, blocking collectives: 50.8 us -> none  [local(): lax.all_to_all(grad_part, 'route', split_axis=0, concat_axis=0, tiled=True)]
    all_to_all x2 -> x0, waiting for transfers between devices: 47.4 us -> none  [the longest x1 47.4 us: local(): lax.all_to_all(token_part, 'route', split_axis=0, concat_axis=0, tiled=True)]
    ppermute x0 -> x36, starting transfers between devices: none -> 39.4 us  [swap(): return lax.ppermute(x, self.axis, pairs)]
    all_gather x2 -> x0, waiting for transfers between devices: 25.7 us -> none  [the longest x1 25.6 us: local(): lax.all_gather(hidden_cols, 'cuts', axis=1, tiled=True)]
    dot_general x10 -> x40, matrix products: 36.3 us -> 23.9 us  [the longest x8 7.19 us: dense_layer(): lax.dot_general(cot_slots[m][h], column_block(down, columns[m], width), L...]
    gather x4 -> x0, local copies, waits for them, and re-layouts: 11.2 us -> none  [the longest x2 8.77 us: fill_slots(): return jnp.take(padded, owners, axis=0)]
  transfers between devices with their start and end apart: 7 -> 36, of which waited for: 5 -> 15; matrix products, arithmetic and copies ran while one was open for 16% -> 21% of each run, Pallas kernels for 0% -> 6%
where the time goes in v1:
time: 149 us
  waiting for transfers between devices  66.5 us (45%)
  starting transfers between devices  39.4 us (26%)
  matrix products  23.9 us (16%)
  Pallas kernels  9.11 us (6%)
  other arithmetic  5.71 us (4%)
  local copies, waits for them, and re-layouts  3.21 us (2%)
    ppermute x36, waiting for transfers between devices, swap(): return lax.ppermute(x, self.axis, pairs)  66.5 us
    ppermute x36, starting transfers between devices, swap(): return lax.ppermute(x, self.axis, pairs)  39.4 us
    pallas_call x2, Pallas kernels, projecting(): pl.pallas_call(kernel, out_shape=shapes, in_specs=[whole] * len(args) + [...  9.11 us
    dot_general x8, matrix products, dense_layer(): lax.dot_general(cot_slots[m][h], column_block(down, columns[m], width), L...  7.19 us
    dot_general x8, matrix products, dense_layer(): jnp.dot(activ[h], column_block(down, columns[m], width), preferred_elemen...  5.87 us
    dot_general x8, matrix products, dense_layer(): lax.dot_general(hid_slots[m][h], column_block(gate, columns[m], width), L...  5.17 us
  transfers between devices with their start and end apart: 36, of which 15 were waited for; matrix products, arithmetic and copies ran while one was open for 21% of the time, Pallas kernels for 6%

profile of v1, /device:TPU:0, one launch (start us, length us, event | category | flops | bytes accessed | tf_op | source)
XLA Modules:
  0.0 149.1 jit_solution(16537549016430904031)
XLA Ops:
  0.6 3.1 %collective-permute-start.27 = (bf16[128,1024]{1,0:T(8,128)(2,1)}, bf16[128,1024]{1,0:T(8,128)(2,1)}, u32[]{:S(2)}, u32[]{:S(2)}) collective-permute-start(bf16[128,1024]{1,0:T(8,128)(2,1)} %param.18), channel_id=1, source_target_pairs={{0,8},{4,12},{8,0},{12,4},{1,9},{5,13},{9,1},{13,5},{2,10},{6,14},... | collective-permute-start | bytes 786440 | tf_op jit(solution)/shard_map/ppermute | solution.py:120
  3.7 2.6 %collective-permute-start.28 = (bf16[128,1024]{1,0:T(8,128)(2,1)}, bf16[128,1024]{1,0:T(8,128)(2,1)}, u32[]{:S(2)}, u32[]{:S(2)}) collective-permute-start(bf16[128,1024]{1,0:T(8,128)(2,1)} %param.18), channel_id=1, source_target_pairs={{0,2},{1,3},{2,0},{3,1},{4,6},{5,7},{6,4},{7,5},{8,10},{9,11},{10,... | collective-permute-start | bytes 786440 | tf_op jit(solution)/shard_map/ppermute | solution.py:120
  6.3 3.8 %shard_map.139 = (bf16[128,1024]{1,0:T(8,128)(2,1)}, bf16[128,1024]{1,0:T(8,128)(2,1)}) custom-call(bf16[128,1024]{1,0:T(8,128)(2,1)} %q_ref.1, bf16[128,256]{1,0:T(8,128)(2,1)} %k_ref.1, bf16[128,256]{1,0:T(8,128)(2,1)} %v_ref.1, bf16[1024,4096]{1,0:T(8,128)(2,1)} %w_hbm.3), custom_call_target="tpu_custom_call" | custom-call | flops 335544320 | bytes 2097152 | tf_op jit(solution)/shard_map/pallas_call | solution.py:68
  10.1 5.3 %shard_map.140 = (bf16[128,1024]{1,0:T(8,128)(2,1)}, bf16[128,1024]{1,0:T(8,128)(2,1)}, f32[128,1024]{1,0:T(8,128)}) custom-call(bf16[128,1024]{1,0:T(8,128)(2,1)} %get-tuple-element.18.att, bf16[128,1024]{1,0:T(8,128)(2,1)} %r_ref.1, bf16[1024,4096]{1,0:T(8,128)(2,1)} %w_hbm.3), custom_call_target="tpu_custom_call" | custom-call | flops 805306368 | bytes 6291456 | tf_op jit(solution)/shard_map/pallas_call | solution.py:68
  15.5 1.6 %collective-permute-start.2 = (bf16[128,1024]{1,0:T(8,128)(2,1)}, bf16[128,1024]{1,0:T(8,128)(2,1)}, u32[]{:S(2)}, u32[]{:S(2)}) collective-permute-start(bf16[128,1024]{1,0:T(8,128)(2,1)} %get-tuple-element.22), channel_id=1, source_target_pairs={{0,1},{1,0},{2,3},{3,2},{4,5},{5,4},{6,7},{7,6},{8,9},{9,8},{10,11... | collective-permute-start | bytes 786440 | tf_op jit(solution)/shard_map/ppermute | solution.py:120
  19.1 2.1 %collective-permute-done.3 = f32[1,4,128]{2,1,0:T(4,128)S(1)} collective-permute-done((f32[1,4,128]{2,1,0:T(4,128)S(1)}, f32[1,4,128]{2,1,0:T(4,128)S(1)}, u32[]{:S(2)}, u32[]{:S(2)}) %collective-permute-start.3) | collective-permute-done | bytes 2080 | tf_op jit(solution)/shard_map/ppermute | solution.py:120
  22.4 7.2 %collective-permute-done = bf16[128,1024]{1,0:T(8,128)(2,1)} collective-permute-done((bf16[128,1024]{1,0:T(8,128)(2,1)}, bf16[128,1024]{1,0:T(8,128)(2,1)}, u32[]{:S(2)}, u32[]{:S(2)}) %collective-permute-start) | collective-permute-done | bytes 262176 | tf_op jit(solution)/shard_map/ppermute | solution.py:120
  30.8 1.6 %collective-permute-start.1 = (bf16[128,1024]{1,0:T(8,128)(2,1)S(1)}, bf16[128,1024]{1,0:T(8,128)(2,1)S(1)}, u32[]{:S(2)}, u32[]{:S(2)}) collective-permute-start(bf16[128,1024]{1,0:T(8,128)(2,1)S(1)} %add_convert_fusion.11), channel_id=1, source_target_pairs={{0,2},{1,3},{2,0},{3,1},{4,6},{5,7},{6,4},{7,5},{8,10},{9,11},{10,... | collective-permute-start | bytes 786440 | tf_op jit(solution)/shard_map/ppermute | solution.py:120
  34.1 2.4 %fusion.26 = f32[256,800]{0,1:T(8,128)S(1)} fusion(bf16[256,1024]{1,0:T(8,128)(2,1)S(1)} %constant_dynamic-update-slice_fusion.6, bf16[1,800,4096]{2,1,0:T(8,128)(2,1)} %param.22, s32[]{:T(128)S(6)} %select_n.29), kind=kOutput, calls=%fused_computation.26 | convolution fusion | flops 419430400 | bytes 2981892 | tf_op jit(solution)/shard_map/dot_general | solution.py:213
  37.5 7.1 %collective-permute-done.1 = bf16[128,1024]{1,0:T(8,128)(2,1)S(1)} collective-permute-done((bf16[128,1024]{1,0:T(8,128)(2,1)S(1)}, bf16[128,1024]{1,0:T(8,128)(2,1)S(1)}, u32[]{:S(2)}, u32[]{:S(2)}) %collective-permute-start.1) | collective-permute-done | bytes 262176 | tf_op jit(solution)/shard_map/ppermute | solution.py:120
  47.1 3.4 %collective-permute-start.5 = (bf16[128,1024]{1,0:T(8,128)(2,1)S(1)}, bf16[128,1024]{1,0:T(8,128)(2,1)S(1)}, u32[]{:S(2)}, u32[]{:S(2)}) collective-permute-start(bf16[128,1024]{1,0:T(8,128)(2,1)S(1)} %add_convert_fusion.10), channel_id=1, source_target_pairs={{0,2},{1,3},{2,0},{3,1},{4,6},{5,7},{6,4},{7,5},{8,10},{9,11},{10,... | collective-permute-start | bytes 786440 | tf_op jit(solution)/shard_map/ppermute | solution.py:120
  52.3 5.9 %collective-permute-done.7 = bf16[128,1024]{1,0:T(8,128)(2,1)S(1)} collective-permute-done((bf16[128,1024]{1,0:T(8,128)(2,1)S(1)}, bf16[128,1024]{1,0:T(8,128)(2,1)S(1)}, u32[]{:S(2)}, u32[]{:S(2)}) %collective-permute-start.7) | collective-permute-done | bytes 262176 | tf_op jit(solution)/shard_map/ppermute | solution.py:120
  58.4 3.7 %collective-permute-done.5 = bf16[128,1024]{1,0:T(8,128)(2,1)S(1)} collective-permute-done((bf16[128,1024]{1,0:T(8,128)(2,1)S(1)}, bf16[128,1024]{1,0:T(8,128)(2,1)S(1)}, u32[]{:S(2)}, u32[]{:S(2)}) %collective-permute-start.5) | collective-permute-done | bytes 262176 | tf_op jit(solution)/shard_map/ppermute | solution.py:120
  66.3 4.0 %collective-permute-done.6 = bf16[128,1024]{1,0:T(8,128)(2,1)S(1)} collective-permute-done((bf16[128,1024]{1,0:T(8,128)(2,1)S(1)}, bf16[128,1024]{1,0:T(8,128)(2,1)S(1)}, u32[]{:S(2)}, u32[]{:S(2)}) %collective-permute-start.6) | collective-permute-done | bytes 262176 | tf_op jit(solution)/shard_map/ppermute | solution.py:120
  70.3 2.0 %collective-permute-start.12 = (bf16[128,1024]{1,0:T(8,128)(2,1)S(1)}, bf16[128,1024]{1,0:T(8,128)(2,1)S(1)}, u32[]{:S(2)}, u32[]{:S(2)}) collective-permute-start(bf16[128,1024]{1,0:T(8,128)(2,1)S(1)} %collective-permute-done.5), channel_id=1, source_target_pairs={{0,1},{1,0},{2,3},{3,2},{4,5},{5,4},{6,7},{7,6},{8,9},{9,8},{10,11... | collective-permute-start | bytes 786440 | tf_op jit(solution)/shard_map/ppermute | solution.py:120
  75.0 11.8 %collective-permute-done.12 = bf16[128,1024]{1,0:T(8,128)(2,1)S(1)} collective-permute-done((bf16[128,1024]{1,0:T(8,128)(2,1)S(1)}, bf16[128,1024]{1,0:T(8,128)(2,1)S(1)}, u32[]{:S(2)}, u32[]{:S(2)}) %collective-permute-start.12) | collective-permute-done | bytes 262176 | tf_op jit(solution)/shard_map/ppermute | solution.py:120
  88.5 4.7 %collective-permute-done.13 = bf16[128,1024]{1,0:T(8,128)(2,1)S(1)} collective-permute-done((bf16[128,1024]{1,0:T(8,128)(2,1)S(1)}, bf16[128,1024]{1,0:T(8,128)(2,1)S(1)}, u32[]{:S(2)}, u32[]{:S(2)}) %collective-permute-start.13) | collective-permute-done | bytes 262176 | tf_op jit(solution)/shard_map/ppermute | solution.py:120
  113.6 3.2 %collective-permute-done.25 = bf16[128,1024]{1,0:T(8,128)(2,1)S(1)} collective-permute-done((bf16[128,1024]{1,0:T(8,128)(2,1)S(1)}, bf16[128,1024]{1,0:T(8,128)(2,1)S(1)}, u32[]{:S(2)}, u32[]{:S(2)}) %collective-permute-start.25) | collective-permute-done | bytes 262176 | tf_op jit(solution)/shard_map/ppermute | solution.py:120
  116.8 2.4 %collective-permute-start.26 = (bf16[128,1024]{1,0:T(8,128)(2,1)S(1)}, bf16[128,1024]{1,0:T(8,128)(2,1)S(1)}, u32[]{:S(2)}, u32[]{:S(2)}) collective-permute-start(bf16[128,1024]{1,0:T(8,128)(2,1)S(1)} %add_convert_fusion.5), channel_id=1, source_target_pairs={{0,1},{1,0},{2,3},{3,2},{4,5},{5,4},{6,7},{7,6},{8,9},{9,8},{10,11... | collective-permute-start | bytes 786440 | tf_op jit(solution)/shard_map/ppermute | solution.py:120
  122.4 2.4 %collective-permute-start.22 = (bf16[128,1024]{1,0:T(8,128)(2,1)S(1)}, bf16[128,1024]{1,0:T(8,128)(2,1)S(1)}, u32[]{:S(2)}, u32[]{:S(2)}) collective-permute-start(bf16[128,1024]{1,0:T(8,128)(2,1)S(1)} %add_convert_fusion.7), channel_id=1, source_target_pairs={{0,1},{1,0},{2,3},{3,2},{4,5},{5,4},{6,7},{7,6},{8,9},{9,8},{10,11... | collective-permute-start | bytes 786440 | tf_op jit(solution)/shard_map/ppermute | solution.py:120
  124.8 2.1 %collective-permute-done.34 = bf16[128,256]{1,0:T(8,128)(2,1)S(1)} collective-permute-done((bf16[128,256]{1,0:T(8,128)(2,1)S(1)}, bf16[128,256]{1,0:T(8,128)(2,1)S(1)}, u32[]{:S(2)}, u32[]{:S(2)}) %collective-permute-start.34) | collective-permute-done | bytes 65568 | tf_op jit(solution)/shard_map/ppermute | solution.py:120
  127.0 5.4 %collective-permute-start.35 = (bf16[128,256]{1,0:T(8,128)(2,1)S(1)}, bf16[128,256]{1,0:T(8,128)(2,1)S(1)}, u32[]{:S(2)}, u32[]{:S(2)}) collective-permute-start(bf16[128,256]{1,0:T(8,128)(2,1)S(1)} %add_convert_fusion.13), channel_id=1, source_target_pairs={{0,2},{1,3},{2,0},{3,1},{4,6},{5,7},{6,4},{7,5},{8,10},{9,11},{10,... | collective-permute-start | bytes 196616 | tf_op jit(solution)/shard_map/ppermute | solution.py:120
  134.9 2.9 %collective-permute-start.23 = (bf16[128,1024]{1,0:T(8,128)(2,1)S(1)}, bf16[128,1024]{1,0:T(8,128)(2,1)S(1)}, u32[]{:S(2)}, u32[]{:S(2)}) collective-permute-start(bf16[128,1024]{1,0:T(8,128)(2,1)S(1)} %add_convert_fusion.6), channel_id=1, source_target_pairs={{0,2},{1,3},{2,0},{3,1},{4,6},{5,7},{6,4},{7,5},{8,10},{9,11},{10,... | collective-permute-start | bytes 786440 | tf_op jit(solution)/shard_map/ppermute | solution.py:120
  139.0 9.3 %collective-permute-done.23 = bf16[128,1024]{1,0:T(8,128)(2,1)S(1)} collective-permute-done((bf16[128,1024]{1,0:T(8,128)(2,1)S(1)}, bf16[128,1024]{1,0:T(8,128)(2,1)S(1)}, u32[]{:S(2)}, u32[]{:S(2)}) %collective-permute-start.23) | collective-permute-done | bytes 262176 | tf_op jit(solution)/shard_map/ppermute | solution.py:120
  (140 shorter events, 47.8 us)
Async XLA Ops:
  0.6 31.8 %collective-permute-start.27 = (bf16[128,1024]{1,0:T(8,128)(2,1)}, bf16[128,1024]{1,0:T(8,128)(2,1)}, u32[]{:S(2)}, u32[]{:S(2)}) collective-permute-start(bf16[128,1024]{1,0:T(8,128)(2,1)} %param.18), channel_id=1, source_target_pairs={{0,8},{4,12},{8,0},{12,4},{1,9},{5,13},{9,1},{13,5},{2,10},{6,14},... | collective-permute-start | bytes 786440 | tf_op jit(solution)/shard_map/ppermute | solution.py:120
  3.7 29.8 %collective-permute-start.28 = (bf16[128,1024]{1,0:T(8,128)(2,1)}, bf16[128,1024]{1,0:T(8,128)(2,1)}, u32[]{:S(2)}, u32[]{:S(2)}) collective-permute-start(bf16[128,1024]{1,0:T(8,128)(2,1)} %param.18), channel_id=1, source_target_pairs={{0,2},{1,3},{2,0},{3,1},{4,6},{5,7},{6,4},{7,5},{8,10},{9,11},{10,... | collective-permute-start | bytes 786440 | tf_op jit(solution)/shard_map/ppermute | solution.py:120
  15.5 22.0 %collective-permute-start.2 = (bf16[128,1024]{1,0:T(8,128)(2,1)}, bf16[128,1024]{1,0:T(8,128)(2,1)}, u32[]{:S(2)}, u32[]{:S(2)}) collective-permute-start(bf16[128,1024]{1,0:T(8,128)(2,1)} %get-tuple-element.22), channel_id=1, source_target_pairs={{0,1},{1,0},{2,3},{3,2},{4,5},{5,4},{6,7},{7,6},{8,9},{9,8},{10,11... | collective-permute-start | bytes 786440 | tf_op jit(solution)/shard_map/ppermute | solution.py:120
  17.1 12.5 %collective-permute-start = (bf16[128,1024]{1,0:T(8,128)(2,1)}, bf16[128,1024]{1,0:T(8,128)(2,1)}, u32[]{:S(2)}, u32[]{:S(2)}) collective-permute-start(bf16[128,1024]{1,0:T(8,128)(2,1)} %get-tuple-element.21), channel_id=1, source_target_pairs={{0,1},{1,0},{2,3},{3,2},{4,5},{5,4},{6,7},{7,6},{8,9},{9,8},{10,11... | collective-permute-start | bytes 786440 | tf_op jit(solution)/shard_map/ppermute | solution.py:120
  30.8 13.8 %collective-permute-start.1 = (bf16[128,1024]{1,0:T(8,128)(2,1)S(1)}, bf16[128,1024]{1,0:T(8,128)(2,1)S(1)}, u32[]{:S(2)}, u32[]{:S(2)}) collective-permute-start(bf16[128,1024]{1,0:T(8,128)(2,1)S(1)} %add_convert_fusion.11), channel_id=1, source_target_pairs={{0,2},{1,3},{2,0},{3,1},{4,6},{5,7},{6,4},{7,5},{8,10},{9,11},{10,... | collective-permute-start | bytes 786440 | tf_op jit(solution)/shard_map/ppermute | solution.py:120
  33.5 40.9 %collective-permute-start.30 = (bf16[256,1024]{1,0:T(8,128)(2,1)S(1)}, bf16[256,1024]{1,0:T(8,128)(2,1)S(1)}, u32[]{:S(2)}, u32[]{:S(2)}) collective-permute-start(bf16[256,1024]{1,0:T(8,128)(2,1)S(1)} %constant_dynamic-update-slice_fusion.6), channel_id=1, source_target_pairs={{0,4},{4,0},{8,12},{12,8},{1,5},{5,1},{9,13},{13,9},{2,6},{6,2},{1... | collective-permute-start | bytes 1572872 | tf_op jit(solution)/shard_map/ppermute | solution.py:120
  33.5 16.9 %collective-permute-start.29 = (bf16[128,1024]{1,0:T(8,128)(2,1)}, bf16[128,1024]{1,0:T(8,128)(2,1)S(1)}, u32[]{:S(2)}, u32[]{:S(2)}) collective-permute-start(bf16[128,1024]{1,0:T(8,128)(2,1)} %collective-permute-done.28), channel_id=1, source_target_pairs={{0,8},{4,12},{8,0},{12,4},{1,9},{5,13},{9,1},{13,5},{2,10},{6,14},... | collective-permute-start | bytes 786440 | tf_op jit(solution)/shard_map/ppermute | solution.py:120
  45.9 12.3 %collective-permute-start.7 = (bf16[128,1024]{1,0:T(8,128)(2,1)S(1)}, bf16[128,1024]{1,0:T(8,128)(2,1)S(1)}, u32[]{:S(2)}, u32[]{:S(2)}) collective-permute-start(bf16[128,1024]{1,0:T(8,128)(2,1)S(1)} %add_convert_fusion.10), channel_id=1, source_target_pairs={{0,1},{1,0},{2,3},{3,2},{4,5},{5,4},{6,7},{7,6},{8,9},{9,8},{10,11... | collective-permute-start | bytes 786440 | tf_op jit(solution)/shard_map/ppermute | solution.py:120
  46.6 11.7 %collective-permute-start.4 = (bf16[128,1024]{1,0:T(8,128)(2,1)S(1)}, bf16[128,1024]{1,0:T(8,128)(2,1)S(1)}, u32[]{:S(2)}, u32[]{:S(2)}) collective-permute-start(bf16[128,1024]{1,0:T(8,128)(2,1)S(1)} %add_convert_fusion.10), channel_id=1, source_target_pairs={{0,8},{4,12},{8,0},{12,4},{1,9},{5,13},{9,1},{13,5},{2,10},{6,14},... | collective-permute-start | bytes 786440 | tf_op jit(solution)/shard_map/ppermute | solution.py:120
  47.1 15.1 %collective-permute-start.5 = (bf16[128,1024]{1,0:T(8,128)(2,1)S(1)}, bf16[128,1024]{1,0:T(8,128)(2,1)S(1)}, u32[]{:S(2)}, u32[]{:S(2)}) collective-permute-start(bf16[128,1024]{1,0:T(8,128)(2,1)S(1)} %add_convert_fusion.10), channel_id=1, source_target_pairs={{0,2},{1,3},{2,0},{3,1},{4,6},{5,7},{6,4},{7,5},{8,10},{9,11},{10,... | collective-permute-start | bytes 786440 | tf_op jit(solution)/shard_map/ppermute | solution.py:120
  50.5 23.2 %collective-permute-start.31 = (bf16[256,1024]{1,0:T(8,128)(2,1)S(1)}, bf16[256,1024]{1,0:T(8,128)(2,1)S(1)}, u32[]{:S(2)}, u32[]{:S(2)}) collective-permute-start(bf16[256,1024]{1,0:T(8,128)(2,1)S(1)} %constant_dynamic-update-slice_fusion.8), channel_id=1, source_target_pairs={{0,4},{4,0},{8,12},{12,8},{1,5},{5,1},{9,13},{13,9},{2,6},{6,2},{1... | collective-permute-start | bytes 1572872 | tf_op jit(solution)/shard_map/ppermute | solution.py:120
  58.2 40.0 %collective-permute-start.32 = (bf16[512,1024]{1,0:T(8,128)(2,1)S(1)}, bf16[512,1024]{1,0:T(8,128)(2,1)S(1)}, u32[]{:S(2)}, u32[]{:S(2)}) collective-permute-start(bf16[512,1024]{1,0:T(8,128)(2,1)S(1)} %pad_maximum_fusion), channel_id=1, source_target_pairs={{0,1},{1,0},{2,3},{3,2},{4,5},{5,4},{6,7},{7,6},{8,9},{9,8},{10,11... | collective-permute-start | bytes 3145736 | tf_op jit(solution)/shard_map/ppermute | solution.py:120
  66.3 28.9 %collective-permute-start.9 = (bf16[256,1024]{1,0:T(8,128)(2,1)S(1)}, bf16[256,1024]{1,0:T(8,128)(2,1)S(1)}, u32[]{:S(2)}, u32[]{:S(2)}) collective-permute-start(bf16[256,1024]{1,0:T(8,128)(2,1)S(1)} %pad_maximum_fusion.1), channel_id=1, source_target_pairs={{0,4},{4,0},{8,12},{12,8},{1,5},{5,1},{9,13},{13,9},{2,6},{6,2},{1... | collective-permute-start | bytes 1572872 | tf_op jit(solution)/shard_map/ppermute | solution.py:120
  70.3 16.5 %collective-permute-start.12 = (bf16[128,1024]{1,0:T(8,128)(2,1)S(1)}, bf16[128,1024]{1,0:T(8,128)(2,1)S(1)}, u32[]{:S(2)}, u32[]{:S(2)}) collective-permute-start(bf16[128,1024]{1,0:T(8,128)(2,1)S(1)} %collective-permute-done.5), channel_id=1, source_target_pairs={{0,1},{1,0},{2,3},{3,2},{4,5},{5,4},{6,7},{7,6},{8,9},{9,8},{10,11... | collective-permute-start | bytes 786440 | tf_op jit(solution)/shard_map/ppermute | solution.py:120
  73.7 19.6 %collective-permute-start.11 = (bf16[256,1024]{1,0:T(8,128)(2,1)S(1)}, bf16[256,1024]{1,0:T(8,128)(2,1)S(1)}, u32[]{:S(2)}, u32[]{:S(2)}) collective-permute-start(bf16[256,1024]{1,0:T(8,128)(2,1)S(1)} %constant_dynamic-update-slice_fusion.2), channel_id=1, source_target_pairs={{0,4},{4,0},{8,12},{12,8},{1,5},{5,1},{9,13},{13,9},{2,6},{6,2},{1... | collective-permute-start | bytes 1572872 | tf_op jit(solution)/shard_map/ppermute | solution.py:120
  74.4 19.2 %collective-permute-start.10 = (bf16[256,1024]{1,0:T(8,128)(2,1)S(1)}, bf16[256,1024]{1,0:T(8,128)(2,1)S(1)}, u32[]{:S(2)}, u32[]{:S(2)}) collective-permute-start(bf16[256,1024]{1,0:T(8,128)(2,1)S(1)} %constant_dynamic-update-slice_fusion), channel_id=1, source_target_pairs={{0,4},{4,0},{8,12},{12,8},{1,5},{5,1},{9,13},{13,9},{2,6},{6,2},{1... | collective-permute-start | bytes 1572872 | tf_op jit(solution)/shard_map/ppermute | solution.py:120
  98.2 21.0 %collective-permute-start.33 = (bf16[512,1024]{1,0:T(8,128)(2,1)S(1)}, bf16[512,1024]{1,0:T(8,128)(2,1)S(1)}, u32[]{:S(2)}, u32[]{:S(2)}) collective-permute-start(bf16[512,1024]{1,0:T(8,128)(2,1)S(1)} %collective-permute-done.32), channel_id=1, source_target_pairs={{0,4},{4,0},{8,12},{12,8},{1,5},{5,1},{9,13},{13,9},{2,6},{6,2},{1... | collective-permute-start | bytes 3145736 | tf_op jit(solution)/shard_map/ppermute | solution.py:120
  107.5 9.2 %collective-permute-start.25 = (bf16[128,1024]{1,0:T(8,128)(2,1)S(1)}, bf16[128,1024]{1,0:T(8,128)(2,1)S(1)}, u32[]{:S(2)}, u32[]{:S(2)}) collective-permute-start(bf16[128,1024]{1,0:T(8,128)(2,1)S(1)} %split.63), channel_id=1, source_target_pairs={{0,8},{4,12},{8,0},{12,4},{1,9},{5,13},{9,1},{13,5},{2,10},{6,14},... | collective-permute-start | bytes 786440 | tf_op jit(solution)/shard_map/ppermute | solution.py:120
  108.5 13.8 %collective-permute-start.21 = (bf16[128,1024]{1,0:T(8,128)(2,1)S(1)}, bf16[128,1024]{1,0:T(8,128)(2,1)S(1)}, u32[]{:S(2)}, u32[]{:S(2)}) collective-permute-start(bf16[128,1024]{1,0:T(8,128)(2,1)S(1)} %split.61), channel_id=1, source_target_pairs={{0,8},{4,12},{8,0},{12,4},{1,9},{5,13},{9,1},{13,5},{2,10},{6,14},... | collective-permute-start | bytes 786440 | tf_op jit(solution)/shard_map/ppermute | solution.py:120
  110.6 24.1 %collective-permute-start.19 = (bf16[128,1024]{1,0:T(8,128)(2,1)S(1)}, bf16[128,1024]{1,0:T(8,128)(2,1)S(1)}, u32[]{:S(2)}, u32[]{:S(2)}) collective-permute-start(bf16[128,1024]{1,0:T(8,128)(2,1)S(1)} %split.59), channel_id=1, source_target_pairs={{0,8},{4,12},{8,0},{12,4},{1,9},{5,13},{9,1},{13,5},{2,10},{6,14},... | collective-permute-start | bytes 786440 | tf_op jit(solution)/shard_map/ppermute | solution.py:120
  112.2 26.7 %collective-permute-start.17 = (bf16[128,1024]{1,0:T(8,128)(2,1)S(1)}, bf16[128,1024]{1,0:T(8,128)(2,1)S(1)}, u32[]{:S(2)}, u32[]{:S(2)}) collective-permute-start(bf16[128,1024]{1,0:T(8,128)(2,1)S(1)} %split.57), channel_id=1, source_target_pairs={{0,8},{4,12},{8,0},{12,4},{1,9},{5,13},{9,1},{13,5},{2,10},{6,14},... | collective-permute-start | bytes 786440 | tf_op jit(solution)/shard_map/ppermute | solution.py:120
  116.8 22.2 %collective-permute-start.26 = (bf16[128,1024]{1,0:T(8,128)(2,1)S(1)}, bf16[128,1024]{1,0:T(8,128)(2,1)S(1)}, u32[]{:S(2)}, u32[]{:S(2)}) collective-permute-start(bf16[128,1024]{1,0:T(8,128)(2,1)S(1)} %add_convert_fusion.5), channel_id=1, source_target_pairs={{0,1},{1,0},{2,3},{3,2},{4,5},{5,4},{6,7},{7,6},{8,9},{9,8},{10,11... | collective-permute-start | bytes 786440 | tf_op jit(solution)/shard_map/ppermute | solution.py:120
  122.4 12.4 %collective-permute-start.22 = (bf16[128,1024]{1,0:T(8,128)(2,1)S(1)}, bf16[128,1024]{1,0:T(8,128)(2,1)S(1)}, u32[]{:S(2)}, u32[]{:S(2)}) collective-permute-start(bf16[128,1024]{1,0:T(8,128)(2,1)S(1)} %add_convert_fusion.7), channel_id=1, source_target_pairs={{0,1},{1,0},{2,3},{3,2},{4,5},{5,4},{6,7},{7,6},{8,9},{9,8},{10,11... | collective-permute-start | bytes 786440 | tf_op jit(solution)/shard_map/ppermute | solution.py:120
  134.9 13.3 %collective-permute-start.23 = (bf16[128,1024]{1,0:T(8,128)(2,1)S(1)}, bf16[128,1024]{1,0:T(8,128)(2,1)S(1)}, u32[]{:S(2)}, u32[]{:S(2)}) collective-permute-start(bf16[128,1024]{1,0:T(8,128)(2,1)S(1)} %add_convert_fusion.6), channel_id=1, source_target_pairs={{0,2},{1,3},{2,0},{3,1},{4,6},{5,7},{6,4},{7,5},{8,10},{9,11},{10,... | collective-permute-start | bytes 786440 | tf_op jit(solution)/shard_map/ppermute | solution.py:120
  (20 other events, 267.8 us)

commit v2 on v1

--- a/solution.py
+++ b/solution.py
@@ -12,22 +12,29 @@
 ADAPTER_SCALE = 0.5
 F32 = jnp.float32
 BF16 = jnp.bfloat16
+COPY_PIECES = 8
 LAST = (((1,), (1,)), ((), ()))
 FIRST = (((0,), (0,)), ((), ()))
 
 
 def fetch(blocks, w_hbm, wbuf, sems):
     copies = []
+    pieces, (_, depth, width) = sems.shape[1], wbuf.shape
     for i, block in enumerate(blocks):
-        width = wbuf.shape[2]
         columns = pl.ds(pl.multiple_of(block * width, width), width)
-        copies.append(pltpu.make_async_copy(w_hbm.at[:, columns], wbuf.at[i], sems.at[i]))
-        copies[-1].start()
+        copies.append([])
+        for j in range(pieces):
+            rows = pl.ds(j * (depth // pieces), depth // pieces)
+            copy = pltpu.make_async_copy(
+                w_hbm.at[rows, columns], wbuf.at[i, rows], sems.at[i, j]
+            )
+            copy.start()
+            copies[i].append(copy)
     return copies
 
 
 def attend_kernel(across, q_ref, k_ref, v_ref, w_hbm, att, out, wbuf, sems):
-    (copy,) = fetch(across.blocks()[-1:], w_hbm, wbuf, sems)
+    (copies,) = fetch(across.blocks()[-1:], w_hbm, wbuf, sems)
     length = q_ref.shape[0]
     per_kv = q_ref.shape[1] // k_ref.shape[1]
     rows = per_kv * length
@@ -46,7 +53,8 @@
         got = jnp.dot(weights, v_ref[:, lanes], preferred_element_type=F32).astype(BF16)
         for i, h in enumerate(heads):
             att[:, h] = got[i * length : (i + 1) * length]
-    copy.wait()
+    for copy in copies:
+        copy.wait()
     out[...] = jnp.dot(att[...], wbuf[0], preferred_element_type=F32).astype(out.dtype)
 
 
@@ -55,7 +63,8 @@
     blocks = across.blocks()
     copies = fetch([blocks[m] for m in slots], w_hbm, wbuf, sems)
     for i, m in enumerate(slots):
-        copies[i].wait()
+        for copy in copies[i]:
+            copy.wait()
         term = jnp.dot(att[...], wbuf[i], preferred_element_type=F32)
         if m == 0:
             term = term + r_ref[...].astype(F32)
@@ -64,7 +73,7 @@
 
 def projecting(kernel, outs, args, matrix, slots, width, flops):
     whole = pl.BlockSpec(memory_space=pltpu.VMEM)
-    shapes = [jax.ShapeDtypeStruct(shape, dtype) for shape, dtype in outs]
+    shapes = [pltpu.VMEM(shape, dtype) for shape, dtype in outs]
     return pl.pallas_call(
         kernel,
         out_shape=shapes,
@@ -72,7 +81,7 @@
         out_specs=[whole] * len(outs),
         scratch_shapes=[
             pltpu.VMEM((slots, matrix.shape[0], width), BF16),
-            pltpu.SemaphoreType.DMA((slots,)),
+            pltpu.SemaphoreType.DMA((slots, COPY_PIECES)),
         ],
         cost_estimate=pl.CostEstimate(
             flops=flops, bytes_accessed=2 * slots * matrix.shape[0] * width, transcendentals=0

time: 149 us -> 148 us (level)
  waiting for transfers between devices: 66.5 us -> 76.1 us
  starting transfers between devices: 39.4 us -> 33.9 us
  other arithmetic: 5.71 us -> 3.48 us
  local copies, waits for them, and re-layouts: 3.21 us -> 1 us
  Pallas kernels: 9.11 us -> 7.57 us
    ppermute x36, waiting for transfers between devices: 66.5 us -> 76.1 us  [swap(): return lax.ppermute(x, self.axis, pairs)]
    ppermute x36, starting transfers between devices: 39.4 us -> 33.9 us  [swap(): return lax.ppermute(x, self.axis, pairs)]
    pallas_call x2, Pallas kernels: 9.11 us -> 7.57 us  [projecting(): pl.pallas_call(kernel, out_shape=shapes, in_specs=[whole] * len(args) + [...]
  transfers between devices with their start and end apart: 36 -> 36, of which waited for: 15 -> 15; matrix products, arithmetic and copies ran while one was open for 21% -> 19% of each run, Pallas kernels for 6% -> 5%
where the time goes in v2:
time: 148 us
  waiting for transfers between devices  76.1 us (51%)
  starting transfers between devices  33.9 us (23%)
  matrix products  24.8 us (17%)
  Pallas kernels  7.57 us (5%)
  other arithmetic  3.48 us (2%)
    ppermute x36, waiting for transfers between devices, swap(): return lax.ppermute(x, self.axis, pairs)  76.1 us
    ppermute x36, starting transfers between devices, swap(): return lax.ppermute(x, self.axis, pairs)  33.9 us
    pallas_call x2, Pallas kernels, projecting(): pl.pallas_call(kernel, out_shape=shapes, in_specs=[whole] * len(args) + [...  7.57 us
    dot_general x8, matrix products, dense_layer(): lax.dot_general(cot_slots[m][h], column_block(down, columns[m], width), L...  6.68 us
    dot_general x8, matrix products, dense_layer(): lax.dot_general(hid_slots[m][h], column_block(gate, columns[m], width), L...  6.59 us
    dot_general x8, matrix products, dense_layer(): jnp.dot(activ[h], column_block(down, columns[m], width), preferred_elemen...  5.88 us
  transfers between devices with their start and end apart: 36, of which 15 were waited for; matrix products, arithmetic and copies ran while one was open for 19% of the time, Pallas kernels for 5%

profile of v2, /device:TPU:0, one launch (start us, length us, event | category | flops | bytes accessed | tf_op | source)
XLA Modules:
  0.0 148.2 jit_solution(2995510693366053557)
XLA Ops:
  0.6 3.1 %collective-permute-start.27 = (bf16[128,1024]{1,0:T(8,128)(2,1)}, bf16[128,1024]{1,0:T(8,128)(2,1)S(1)}, u32[]{:S(2)}, u32[]{:S(2)}) collective-permute-start(bf16[128,1024]{1,0:T(8,128)(2,1)} %param.18), channel_id=1, source_target_pairs={{0,8},{4,12},{8,0},{12,4},{1,9},{5,13},{9,1},{13,5},{2,10},{6,14},... | collective-permute-start | bytes 786440 | tf_op jit(solution)/shard_map/ppermute | solution.py:129
  3.7 2.6 %collective-permute-start.28 = (bf16[128,1024]{1,0:T(8,128)(2,1)}, bf16[128,1024]{1,0:T(8,128)(2,1)S(1)}, u32[]{:S(2)}, u32[]{:S(2)}) collective-permute-start(bf16[128,1024]{1,0:T(8,128)(2,1)} %param.18), channel_id=1, source_target_pairs={{0,2},{1,3},{2,0},{3,1},{4,6},{5,7},{6,4},{7,5},{8,10},{9,11},{10,... | collective-permute-start | bytes 786440 | tf_op jit(solution)/shard_map/ppermute | solution.py:129
  6.3 3.1 %shard_map.139 = (bf16[128,1024]{1,0:T(8,128)(2,1)S(1)}, bf16[128,1024]{1,0:T(8,128)(2,1)S(1)}) custom-call(bf16[128,1024]{1,0:T(8,128)(2,1)} %q_ref.1, bf16[128,256]{1,0:T(8,128)(2,1)} %k_ref.1, bf16[128,256]{1,0:T(8,128)(2,1)} %v_ref.1, bf16[1024,4096]{1,0:T(8,128)(2,1)} %w_hbm.3), custom_call_target="tpu_custom_call" | custom-call | flops 335544320 | bytes 2097152 | tf_op jit(solution)/shard_map/pallas_call | solution.py:77
  10.1 4.5 %shard_map.140 = (bf16[128,1024]{1,0:T(8,128)(2,1)S(1)}, bf16[128,1024]{1,0:T(8,128)(2,1)S(1)}, f32[128,1024]{1,0:T(8,128)S(1)}) custom-call(bf16[128,1024]{1,0:T(8,128)(2,1)} %copy-done.1, bf16[128,1024]{1,0:T(8,128)(2,1)} %r_ref.1, bf16[1024,4096]{1,0:T(8,128)(2,1)} %w_hbm.3), custom_call_target="tpu_custom_call" | custom-call | flops 805306368 | bytes 6291456 | tf_op jit(solution)/shard_map/pallas_call | solution.py:77
  17.3 3.0 %collective-permute-done.3 = f32[1,4,128]{2,1,0:T(4,128)S(1)} collective-permute-done((f32[1,4,128]{2,1,0:T(4,128)S(1)}, f32[1,4,128]{2,1,0:T(4,128)S(1)}, u32[]{:S(2)}, u32[]{:S(2)}) %collective-permute-start.3) | collective-permute-done | bytes 2080 | tf_op jit(solution)/shard_map/ppermute | solution.py:129
  21.5 8.0 %collective-permute-done = bf16[128,1024]{1,0:T(8,128)(2,1)} collective-permute-done((bf16[128,1024]{1,0:T(8,128)(2,1)S(1)}, bf16[128,1024]{1,0:T(8,128)(2,1)}, u32[]{:S(2)}, u32[]{:S(2)}) %collective-permute-start) | collective-permute-done | bytes 262176 | tf_op jit(solution)/shard_map/ppermute | solution.py:129
  32.9 2.1 %fusion.26 = f32[256,800]{0,1:T(8,128)S(1)} fusion(bf16[256,1024]{1,0:T(8,128)(2,1)S(1)} %constant_dynamic-update-slice_fusion.6, bf16[1,800,4096]{2,1,0:T(8,128)(2,1)} %param.22, s32[]{:T(128)S(6)} %select_n.29), kind=kOutput, calls=%fused_computation.26 | convolution fusion | flops 419430400 | bytes 2981892 | tf_op jit(solution)/shard_map/dot_general | solution.py:222
  35.0 10.5 %collective-permute-done.1 = bf16[128,1024]{1,0:T(8,128)(2,1)S(1)} collective-permute-done((bf16[128,1024]{1,0:T(8,128)(2,1)S(1)}, bf16[128,1024]{1,0:T(8,128)(2,1)S(1)}, u32[]{:S(2)}, u32[]{:S(2)}) %collective-permute-start.1) | collective-permute-done | bytes 262176 | tf_op jit(solution)/shard_map/ppermute | solution.py:129
  46.3 2.9 %collective-permute-start.5 = (bf16[128,1024]{1,0:T(8,128)(2,1)S(1)}, bf16[128,1024]{1,0:T(8,128)(2,1)S(1)}, u32[]{:S(2)}, u32[]{:S(2)}) collective-permute-start(bf16[128,1024]{1,0:T(8,128)(2,1)S(1)} %add_convert_fusion.10), channel_id=1, source_target_pairs={{0,2},{1,3},{2,0},{3,1},{4,6},{5,7},{6,4},{7,5},{8,10},{9,11},{10,... | collective-permute-start | bytes 786440 | tf_op jit(solution)/shard_map/ppermute | solution.py:129
  50.0 8.3 %collective-permute-done.7 = bf16[128,1024]{1,0:T(8,128)(2,1)S(1)} collective-permute-done((bf16[128,1024]{1,0:T(8,128)(2,1)S(1)}, bf16[128,1024]{1,0:T(8,128)(2,1)S(1)}, u32[]{:S(2)}, u32[]{:S(2)}) %collective-permute-start.7) | collective-permute-done | bytes 262176 | tf_op jit(solution)/shard_map/ppermute | solution.py:129
  58.4 2.4 %collective-permute-done.5 = bf16[128,1024]{1,0:T(8,128)(2,1)S(1)} collective-permute-done((bf16[128,1024]{1,0:T(8,128)(2,1)S(1)}, bf16[128,1024]{1,0:T(8,128)(2,1)S(1)}, u32[]{:S(2)}, u32[]{:S(2)}) %collective-permute-start.5) | collective-permute-done | bytes 262176 | tf_op jit(solution)/shard_map/ppermute | solution.py:129
  62.7 2.1 %fusion.46 = f32[256,800]{0,1:T(8,128)S(1)} fusion(bf16[1,800,4096]{2,1,0:T(8,128)(2,1)} %param.21, s32[]{:T(128)S(6)} %select_n.29, bf16[128,1024]{1,0:T(8,128)(2,1)S(1)} %collective-permute-done.4, bf16[128,1024]{1,0:T(8,128)(2,1)S(1)} %add_convert_fusion.10), kind=kOutput, calls=%fused_computation.46 | convolution fusion | flops 420478976 | bytes 2981892 | tf_op jit(solution)/shard_map/dot_general | solution.py:225
  64.8 2.8 %collective-permute-done.8 = bf16[128,1024]{1,0:T(8,128)(2,1)S(1)} collective-permute-done((bf16[128,1024]{1,0:T(8,128)(2,1)S(1)}, bf16[128,1024]{1,0:T(8,128)(2,1)S(1)}, u32[]{:S(2)}, u32[]{:S(2)}) %collective-permute-start.8) | collective-permute-done | bytes 262176 | tf_op jit(solution)/shard_map/ppermute | solution.py:129
  67.6 3.0 %collective-permute-done.6 = bf16[128,1024]{1,0:T(8,128)(2,1)S(1)} collective-permute-done((bf16[128,1024]{1,0:T(8,128)(2,1)S(1)}, bf16[128,1024]{1,0:T(8,128)(2,1)S(1)}, u32[]{:S(2)}, u32[]{:S(2)}) %collective-permute-start.6) | collective-permute-done | bytes 262176 | tf_op jit(solution)/shard_map/ppermute | solution.py:129
  70.5 1.7 %collective-permute-start.12 = (bf16[128,1024]{1,0:T(8,128)(2,1)S(1)}, bf16[128,1024]{1,0:T(8,128)(2,1)S(1)}, u32[]{:S(2)}, u32[]{:S(2)}) collective-permute-start(bf16[128,1024]{1,0:T(8,128)(2,1)S(1)} %collective-permute-done.5), channel_id=1, source_target_pairs={{0,1},{1,0},{2,3},{3,2},{4,5},{5,4},{6,7},{7,6},{8,9},{9,8},{10,11... | collective-permute-start | bytes 786440 | tf_op jit(solution)/shard_map/ppermute | solution.py:129
  74.9 12.8 %collective-permute-done.12 = bf16[128,1024]{1,0:T(8,128)(2,1)S(1)} collective-permute-done((bf16[128,1024]{1,0:T(8,128)(2,1)S(1)}, bf16[128,1024]{1,0:T(8,128)(2,1)S(1)}, u32[]{:S(2)}, u32[]{:S(2)}) %collective-permute-start.12) | collective-permute-done | bytes 262176 | tf_op jit(solution)/shard_map/ppermute | solution.py:129
  89.4 4.7 %collective-permute-done.13 = bf16[128,1024]{1,0:T(8,128)(2,1)S(1)} collective-permute-done((bf16[128,1024]{1,0:T(8,128)(2,1)S(1)}, bf16[128,1024]{1,0:T(8,128)(2,1)S(1)}, u32[]{:S(2)}, u32[]{:S(2)}) %collective-permute-start.13) | collective-permute-done | bytes 262176 | tf_op jit(solution)/shard_map/ppermute | solution.py:129
  114.3 3.2 %collective-permute-done.25 = bf16[128,1024]{1,0:T(8,128)(2,1)S(1)} collective-permute-done((bf16[128,1024]{1,0:T(8,128)(2,1)S(1)}, bf16[128,1024]{1,0:T(8,128)(2,1)S(1)}, u32[]{:S(2)}, u32[]{:S(2)}) %collective-permute-start.25) | collective-permute-done | bytes 262176 | tf_op jit(solution)/shard_map/ppermute | solution.py:129
  119.3 2.1 %collective-permute-start.34 = (bf16[128,256]{1,0:T(8,128)(2,1)S(1)}, bf16[128,256]{1,0:T(8,128)(2,1)S(1)}, u32[]{:S(2)}, u32[]{:S(2)}) collective-permute-start(bf16[128,256]{1,0:T(8,128)(2,1)S(1)} %pad_maximum_fusion.2), channel_id=1, source_target_pairs={{0,1},{1,0},{2,3},{3,2},{4,5},{5,4},{6,7},{7,6},{8,9},{9,8},{10,11... | collective-permute-start | bytes 196616 | tf_op jit(solution)/shard_map/ppermute | solution.py:129
  121.4 1.7 %collective-permute-done.21 = bf16[128,1024]{1,0:T(8,128)(2,1)S(1)} collective-permute-done((bf16[128,1024]{1,0:T(8,128)(2,1)S(1)}, bf16[128,1024]{1,0:T(8,128)(2,1)S(1)}, u32[]{:S(2)}, u32[]{:S(2)}) %collective-permute-start.21) | collective-permute-done | bytes 262176 | tf_op jit(solution)/shard_map/ppermute | solution.py:129
  123.2 3.9 %collective-permute-done.34 = bf16[128,256]{1,0:T(8,128)(2,1)S(1)} collective-permute-done((bf16[128,256]{1,0:T(8,128)(2,1)S(1)}, bf16[128,256]{1,0:T(8,128)(2,1)S(1)}, u32[]{:S(2)}, u32[]{:S(2)}) %collective-permute-start.34) | collective-permute-done | bytes 65568 | tf_op jit(solution)/shard_map/ppermute | solution.py:129
  127.2 4.2 %collective-permute-start.35 = (bf16[128,256]{1,0:T(8,128)(2,1)S(1)}, bf16[128,256]{1,0:T(8,128)(2,1)S(1)}, u32[]{:S(2)}, u32[]{:S(2)}) collective-permute-start(bf16[128,256]{1,0:T(8,128)(2,1)S(1)} %add_convert_fusion.13), channel_id=1, source_target_pairs={{0,2},{1,3},{2,0},{3,1},{4,6},{5,7},{6,4},{7,5},{8,10},{9,11},{10,... | collective-permute-start | bytes 196616 | tf_op jit(solution)/shard_map/ppermute | solution.py:129
  133.9 2.9 %collective-permute-start.23 = (bf16[128,1024]{1,0:T(8,128)(2,1)S(1)}, bf16[128,1024]{1,0:T(8,128)(2,1)S(1)}, u32[]{:S(2)}, u32[]{:S(2)}) collective-permute-start(bf16[128,1024]{1,0:T(8,128)(2,1)S(1)} %add_convert_fusion.6), channel_id=1, source_target_pairs={{0,2},{1,3},{2,0},{3,1},{4,6},{5,7},{6,4},{7,5},{8,10},{9,11},{10,... | collective-permute-start | bytes 786440 | tf_op jit(solution)/shard_map/ppermute | solution.py:129
  138.0 9.2 %collective-permute-done.23 = bf16[128,1024]{1,0:T(8,128)(2,1)S(1)} collective-permute-done((bf16[128,1024]{1,0:T(8,128)(2,1)S(1)}, bf16[128,1024]{1,0:T(8,128)(2,1)S(1)}, u32[]{:S(2)}, u32[]{:S(2)}) %collective-permute-start.23) | collective-permute-done | bytes 262176 | tf_op jit(solution)/shard_map/ppermute | solution.py:129
  (142 shorter events, 42.2 us)
Async XLA Ops:
  0.6 31.6 %collective-permute-start.27 = (bf16[128,1024]{1,0:T(8,128)(2,1)}, bf16[128,1024]{1,0:T(8,128)(2,1)S(1)}, u32[]{:S(2)}, u32[]{:S(2)}) collective-permute-start(bf16[128,1024]{1,0:T(8,128)(2,1)} %param.18), channel_id=1, source_target_pairs={{0,8},{4,12},{8,0},{12,4},{1,9},{5,13},{9,1},{13,5},{2,10},{6,14},... | collective-permute-start | bytes 786440 | tf_op jit(solution)/shard_map/ppermute | solution.py:129
  3.7 28.6 %collective-permute-start.28 = (bf16[128,1024]{1,0:T(8,128)(2,1)}, bf16[128,1024]{1,0:T(8,128)(2,1)S(1)}, u32[]{:S(2)}, u32[]{:S(2)}) collective-permute-start(bf16[128,1024]{1,0:T(8,128)(2,1)} %param.18), channel_id=1, source_target_pairs={{0,2},{1,3},{2,0},{3,1},{4,6},{5,7},{6,4},{7,5},{8,10},{9,11},{10,... | collective-permute-start | bytes 786440 | tf_op jit(solution)/shard_map/ppermute | solution.py:129
  14.6 20.4 %collective-permute-start.2 = (bf16[128,1024]{1,0:T(8,128)(2,1)S(1)}, bf16[128,1024]{1,0:T(8,128)(2,1)S(1)}, u32[]{:S(2)}, u32[]{:S(2)}) collective-permute-start(bf16[128,1024]{1,0:T(8,128)(2,1)S(1)} %get-tuple-element.22), channel_id=1, source_target_pairs={{0,1},{1,0},{2,3},{3,2},{4,5},{5,4},{6,7},{7,6},{8,9},{9,8},{10,11... | collective-permute-start | bytes 786440 | tf_op jit(solution)/shard_map/ppermute | solution.py:129
  16.2 13.3 %collective-permute-start = (bf16[128,1024]{1,0:T(8,128)(2,1)S(1)}, bf16[128,1024]{1,0:T(8,128)(2,1)}, u32[]{:S(2)}, u32[]{:S(2)}) collective-permute-start(bf16[128,1024]{1,0:T(8,128)(2,1)S(1)} %get-tuple-element.21), channel_id=1, source_target_pairs={{0,1},{1,0},{2,3},{3,2},{4,5},{5,4},{6,7},{7,6},{8,9},{9,8},{10,11... | collective-permute-start | bytes 786440 | tf_op jit(solution)/shard_map/ppermute | solution.py:129
  30.7 14.8 %collective-permute-start.1 = (bf16[128,1024]{1,0:T(8,128)(2,1)S(1)}, bf16[128,1024]{1,0:T(8,128)(2,1)S(1)}, u32[]{:S(2)}, u32[]{:S(2)}) collective-permute-start(bf16[128,1024]{1,0:T(8,128)(2,1)S(1)} %add_convert_fusion.11), channel_id=1, source_target_pairs={{0,2},{1,3},{2,0},{3,1},{4,6},{5,7},{6,4},{7,5},{8,10},{9,11},{10,... | collective-permute-start | bytes 786440 | tf_op jit(solution)/shard_map/ppermute | solution.py:129
  32.3 42.1 %collective-permute-start.30 = (bf16[256,1024]{1,0:T(8,128)(2,1)S(1)}, bf16[256,1024]{1,0:T(8,128)(2,1)S(1)}, u32[]{:S(2)}, u32[]{:S(2)}) collective-permute-start(bf16[256,1024]{1,0:T(8,128)(2,1)S(1)} %constant_dynamic-update-slice_fusion.6), channel_id=1, source_target_pairs={{0,4},{4,0},{8,12},{12,8},{1,5},{5,1},{9,13},{13,9},{2,6},{6,2},{1... | collective-permute-start | bytes 1572872 | tf_op jit(solution)/shard_map/ppermute | solution.py:129
  32.4 16.8 %collective-permute-start.29 = (bf16[128,1024]{1,0:T(8,128)(2,1)S(1)}, bf16[128,1024]{1,0:T(8,128)(2,1)S(1)}, u32[]{:S(2)}, u32[]{:S(2)}) collective-permute-start(bf16[128,1024]{1,0:T(8,128)(2,1)S(1)} %collective-permute-done.28), channel_id=1, source_target_pairs={{0,8},{4,12},{8,0},{12,4},{1,9},{5,13},{9,1},{13,5},{2,10},{6,14},... | collective-permute-start | bytes 786440 | tf_op jit(solution)/shard_map/ppermute | solution.py:129
  45.7 12.6 %collective-permute-start.7 = (bf16[128,1024]{1,0:T(8,128)(2,1)S(1)}, bf16[128,1024]{1,0:T(8,128)(2,1)S(1)}, u32[]{:S(2)}, u32[]{:S(2)}) collective-permute-start(bf16[128,1024]{1,0:T(8,128)(2,1)S(1)} %add_convert_fusion.10), channel_id=1, source_target_pairs={{0,1},{1,0},{2,3},{3,2},{4,5},{5,4},{6,7},{7,6},{8,9},{9,8},{10,11... | collective-permute-start | bytes 786440 | tf_op jit(solution)/shard_map/ppermute | solution.py:129
  45.7 12.6 %collective-permute-start.4 = (bf16[128,1024]{1,0:T(8,128)(2,1)S(1)}, bf16[128,1024]{1,0:T(8,128)(2,1)S(1)}, u32[]{:S(2)}, u32[]{:S(2)}) collective-permute-start(bf16[128,1024]{1,0:T(8,128)(2,1)S(1)} %add_convert_fusion.10), channel_id=1, source_target_pairs={{0,8},{4,12},{8,0},{12,4},{1,9},{5,13},{9,1},{13,5},{2,10},{6,14},... | collective-permute-start | bytes 786440 | tf_op jit(solution)/shard_map/ppermute | solution.py:129
  46.3 14.6 %collective-permute-start.5 = (bf16[128,1024]{1,0:T(8,128)(2,1)S(1)}, bf16[128,1024]{1,0:T(8,128)(2,1)S(1)}, u32[]{:S(2)}, u32[]{:S(2)}) collective-permute-start(bf16[128,1024]{1,0:T(8,128)(2,1)S(1)} %add_convert_fusion.10), channel_id=1, source_target_pairs={{0,2},{1,3},{2,0},{3,1},{4,6},{5,7},{6,4},{7,5},{8,10},{9,11},{10,... | collective-permute-start | bytes 786440 | tf_op jit(solution)/shard_map/ppermute | solution.py:129
  49.2 24.5 %collective-permute-start.31 = (bf16[256,1024]{1,0:T(8,128)(2,1)S(1)}, bf16[256,1024]{1,0:T(8,128)(2,1)S(1)}, u32[]{:S(2)}, u32[]{:S(2)}) collective-permute-start(bf16[256,1024]{1,0:T(8,128)(2,1)S(1)} %constant_dynamic-update-slice_fusion.8), channel_id=1, source_target_pairs={{0,4},{4,0},{8,12},{12,8},{1,5},{5,1},{9,13},{13,9},{2,6},{6,2},{1... | collective-permute-start | bytes 1572872 | tf_op jit(solution)/shard_map/ppermute | solution.py:129
  58.3 40.8 %collective-permute-start.32 = (bf16[512,1024]{1,0:T(8,128)(2,1)S(1)}, bf16[512,1024]{1,0:T(8,128)(2,1)S(1)}, u32[]{:S(2)}, u32[]{:S(2)}) collective-permute-start(bf16[512,1024]{1,0:T(8,128)(2,1)S(1)} %pad_maximum_fusion), channel_id=1, source_target_pairs={{0,1},{1,0},{2,3},{3,2},{4,5},{5,4},{6,7},{7,6},{8,9},{9,8},{10,11... | collective-permute-start | bytes 3145736 | tf_op jit(solution)/shard_map/ppermute | solution.py:129
  60.9 9.7 %collective-permute-start.6 = (bf16[128,1024]{1,0:T(8,128)(2,1)S(1)}, bf16[128,1024]{1,0:T(8,128)(2,1)S(1)}, u32[]{:S(2)}, u32[]{:S(2)}) collective-permute-start(bf16[128,1024]{1,0:T(8,128)(2,1)S(1)} %collective-permute-done.5), channel_id=1, source_target_pairs={{0,8},{4,12},{8,0},{12,4},{1,9},{5,13},{9,1},{13,5},{2,10},{6,14},... | collective-permute-start | bytes 786440 | tf_op jit(solution)/shard_map/ppermute | solution.py:129
  67.6 28.5 %collective-permute-start.9 = (bf16[256,1024]{1,0:T(8,128)(2,1)S(1)}, bf16[256,1024]{1,0:T(8,128)(2,1)S(1)}, u32[]{:S(2)}, u32[]{:S(2)}) collective-permute-start(bf16[256,1024]{1,0:T(8,128)(2,1)S(1)} %pad_maximum_fusion.1), channel_id=1, source_target_pairs={{0,4},{4,0},{8,12},{12,8},{1,5},{5,1},{9,13},{13,9},{2,6},{6,2},{1... | collective-permute-start | bytes 1572872 | tf_op jit(solution)/shard_map/ppermute | solution.py:129
  70.5 17.2 %collective-permute-start.12 = (bf16[128,1024]{1,0:T(8,128)(2,1)S(1)}, bf16[128,1024]{1,0:T(8,128)(2,1)S(1)}, u32[]{:S(2)}, u32[]{:S(2)}) collective-permute-start(bf16[128,1024]{1,0:T(8,128)(2,1)S(1)} %collective-permute-done.5), channel_id=1, source_target_pairs={{0,1},{1,0},{2,3},{3,2},{4,5},{5,4},{6,7},{7,6},{8,9},{9,8},{10,11... | collective-permute-start | bytes 786440 | tf_op jit(solution)/shard_map/ppermute | solution.py:129
  73.7 20.6 %collective-permute-start.11 = (bf16[256,1024]{1,0:T(8,128)(2,1)S(1)}, bf16[256,1024]{1,0:T(8,128)(2,1)S(1)}, u32[]{:S(2)}, u32[]{:S(2)}) collective-permute-start(bf16[256,1024]{1,0:T(8,128)(2,1)S(1)} %constant_dynamic-update-slice_fusion.2), channel_id=1, source_target_pairs={{0,4},{4,0},{8,12},{12,8},{1,5},{5,1},{9,13},{13,9},{2,6},{6,2},{1... | collective-permute-start | bytes 1572872 | tf_op jit(solution)/shard_map/ppermute | solution.py:129
  74.4 20.1 %collective-permute-start.10 = (bf16[256,1024]{1,0:T(8,128)(2,1)S(1)}, bf16[256,1024]{1,0:T(8,128)(2,1)S(1)}, u32[]{:S(2)}, u32[]{:S(2)}) collective-permute-start(bf16[256,1024]{1,0:T(8,128)(2,1)S(1)} %constant_dynamic-update-slice_fusion), channel_id=1, source_target_pairs={{0,4},{4,0},{8,12},{12,8},{1,5},{5,1},{9,13},{13,9},{2,6},{6,2},{1... | collective-permute-start | bytes 1572872 | tf_op jit(solution)/shard_map/ppermute | solution.py:129
  99.1 18.5 %collective-permute-start.33 = (bf16[512,1024]{1,0:T(8,128)(2,1)S(1)}, bf16[512,1024]{1,0:T(8,128)(2,1)S(1)}, u32[]{:S(2)}, u32[]{:S(2)}) collective-permute-start(bf16[512,1024]{1,0:T(8,128)(2,1)S(1)} %collective-permute-done.32), channel_id=1, source_target_pairs={{0,4},{4,0},{8,12},{12,8},{1,5},{5,1},{9,13},{13,9},{2,6},{6,2},{1... | collective-permute-start | bytes 3145736 | tf_op jit(solution)/shard_map/ppermute | solution.py:129
  109.0 14.1 %collective-permute-start.21 = (bf16[128,1024]{1,0:T(8,128)(2,1)S(1)}, bf16[128,1024]{1,0:T(8,128)(2,1)S(1)}, u32[]{:S(2)}, u32[]{:S(2)}) collective-permute-start(bf16[128,1024]{1,0:T(8,128)(2,1)S(1)} %split.61), channel_id=1, source_target_pairs={{0,8},{4,12},{8,0},{12,4},{1,9},{5,13},{9,1},{13,5},{2,10},{6,14},... | collective-permute-start | bytes 786440 | tf_op jit(solution)/shard_map/ppermute | solution.py:129
  111.4 22.4 %collective-permute-start.19 = (bf16[128,1024]{1,0:T(8,128)(2,1)S(1)}, bf16[128,1024]{1,0:T(8,128)(2,1)S(1)}, u32[]{:S(2)}, u32[]{:S(2)}) collective-permute-start(bf16[128,1024]{1,0:T(8,128)(2,1)S(1)} %split.59), channel_id=1, source_target_pairs={{0,8},{4,12},{8,0},{12,4},{1,9},{5,13},{9,1},{13,5},{2,10},{6,14},... | collective-permute-start | bytes 786440 | tf_op jit(solution)/shard_map/ppermute | solution.py:129
  112.7 25.3 %collective-permute-start.17 = (bf16[128,1024]{1,0:T(8,128)(2,1)S(1)}, bf16[128,1024]{1,0:T(8,128)(2,1)S(1)}, u32[]{:S(2)}, u32[]{:S(2)}) collective-permute-start(bf16[128,1024]{1,0:T(8,128)(2,1)S(1)} %split.57), channel_id=1, source_target_pairs={{0,8},{4,12},{8,0},{12,4},{1,9},{5,13},{9,1},{13,5},{2,10},{6,14},... | collective-permute-start | bytes 786440 | tf_op jit(solution)/shard_map/ppermute | solution.py:129
  117.5 20.5 %collective-permute-start.26 = (bf16[128,1024]{1,0:T(8,128)(2,1)S(1)}, bf16[128,1024]{1,0:T(8,128)(2,1)S(1)}, u32[]{:S(2)}, u32[]{:S(2)}) collective-permute-start(bf16[128,1024]{1,0:T(8,128)(2,1)S(1)} %add_convert_fusion.5), channel_id=1, source_target_pairs={{0,1},{1,0},{2,3},{3,2},{4,5},{5,4},{6,7},{7,6},{8,9},{9,8},{10,11... | collective-permute-start | bytes 786440 | tf_op jit(solution)/shard_map/ppermute | solution.py:129
  123.2 10.6 %collective-permute-start.22 = (bf16[128,1024]{1,0:T(8,128)(2,1)S(1)}, bf16[128,1024]{1,0:T(8,128)(2,1)S(1)}, u32[]{:S(2)}, u32[]{:S(2)}) collective-permute-start(bf16[128,1024]{1,0:T(8,128)(2,1)S(1)} %add_convert_fusion.7), channel_id=1, source_target_pairs={{0,1},{1,0},{2,3},{3,2},{4,5},{5,4},{6,7},{7,6},{8,9},{9,8},{10,11... | collective-permute-start | bytes 786440 | tf_op jit(solution)/shard_map/ppermute | solution.py:129
  133.9 13.3 %collective-permute-start.23 = (bf16[128,1024]{1,0:T(8,128)(2,1)S(1)}, bf16[128,1024]{1,0:T(8,128)(2,1)S(1)}, u32[]{:S(2)}, u32[]{:S(2)}) collective-permute-start(bf16[128,1024]{1,0:T(8,128)(2,1)S(1)} %add_convert_fusion.6), channel_id=1, source_target_pairs={{0,2},{1,3},{2,0},{3,1},{4,6},{5,7},{6,4},{7,5},{8,10},{9,11},{10,... | collective-permute-start | bytes 786440 | tf_op jit(solution)/shard_map/ppermute | solution.py:129
  (21 other events, 219.2 us)
